TPU v7x, 32 devices: a whole 2x2x4 slice. The times are simulated.
32 devices in a mesh: row: 8 (over y, x, core), col: 4 (over z).
Axes of the slice: x: 2, y: 2, z: 4, core: 2. Of those that a mesh axis runs over, the one named last changes fastest.
Arguments:
- coarse_feats: bfloat16 [64, 512], P(None, ('row', 'col')), may hold values from -6 to 6
- fine_feats: bfloat16 [64, 512], P(None, ('row', 'col')), may hold values from -6 to 6
- pair_prior: bfloat16 [64, 512, 512], P(None, 'row', 'col'), may hold values from -6 to 6
- zoom_start: int32 [2], replicated, may hold values from 0 to 256, as said below
- coarse_weights: bfloat16 [2, 3, 64, 192], replicated, may hold values from -0.25 to 0.25
- coarse_bias: float32 [2, 64], replicated, may hold values from -2.5 to 2.5
- refine_first: bfloat16 [3, 64, 384], replicated, may hold values from -0.1875 to 0.1875
- refine_second: bfloat16 [3, 64, 192], replicated, may hold values from -0.25 to 0.25
- refine_bias: float32 [2, 64], replicated, may hold values from -2.5 to 2.5
Outputs:
- coarse_map: bfloat16 [64, 512, 512], P(None, 'row', 'col')
- refined: bfloat16 [64, 512, 512], P(None, 'row', 'col')
Inputs may be any that keep to these rules, and one draw needn't show every extreme that they name: `zoom_start`: the two entries are 0 and 256 in either order.
All inputs are finite; a program needn't handle non-finite values.
Results may differ from a plain program's by a relative error of at most 0.0059.
Values may be sent and summed in bfloat16 or wider, within the bound.
No kernel may reach another device: no remote copies, remote signals or barrier semaphores. Data moves between devices by JAX's collectives and lax.ppermute only.
A program may use at most 64 MiB of HBM per device.

v0:
```python
import jax
import jax.numpy as jnp
from jax import lax
from jax.sharding import PartitionSpec as P

margin_bins = 24


def with_halo(block, sides, width):
    for axis, dim in sides:
        count = lax.axis_size(axis)
        forward = [(i, i + 1) for i in range(count - 1)]
        backward = [(target, source) for source, target in forward]
        low = lax.ppermute(
            lax.slice_in_dim(block, block.shape[dim] - width, None, axis=dim), axis, forward
        )
        high = lax.ppermute(lax.slice_in_dim(block, 0, width, axis=dim), axis, backward)
        block = jnp.concatenate([low, block, high], axis=dim)
    return block


def conv_valid(padded, weights, spacing, out_rows, out_cols):
    inputs = padded.shape[0]
    outputs = weights.shape[1]
    summed = jnp.zeros((outputs, out_rows * out_cols), jnp.float32)
    for tap_row in range(3):
        strip = padded[:, tap_row * spacing : tap_row * spacing + out_rows, :]
        slices = [
            strip[:, :, tap_col * spacing : tap_col * spacing + out_cols] for tap_col in range(3)
        ]
        if 3 * inputs <= 256:
            stacked = jnp.concatenate(slices, axis=0).reshape(3 * inputs, out_rows * out_cols)
            summed = summed + jnp.dot(weights[tap_row], stacked, preferred_element_type=jnp.float32)
        else:
            for tap_col in range(3):
                kernel = weights[tap_row][:, tap_col * inputs : (tap_col + 1) * inputs]
                summed = summed + jnp.dot(
                    kernel,
                    slices[tap_col].reshape(inputs, out_rows * out_cols),
                    preferred_element_type=jnp.float32,
                )
    return summed.reshape(outputs, out_rows, out_cols)


def conv_layer(padded, weights, biases, spacing, out_rows, out_cols):
    result = conv_valid(padded, weights, spacing, out_rows, out_cols)
    return jnp.maximum(result + biases[:, None, None], 0.0)


def pair_sum(padded_feats, row_first, col_first, row_extent, col_extent):
    row_part = lax.dynamic_slice_in_dim(
        padded_feats, row_first + margin_bins, row_extent, 1
    ).astype(jnp.float32)
    col_part = lax.dynamic_slice_in_dim(
        padded_feats, col_first + margin_bins, col_extent, 1
    ).astype(jnp.float32)
    return row_part[:, :, None] + col_part[:, None, :]


def inside_grid(row_first, col_first, row_extent, col_extent, bins_side):
    row_ids = row_first + jnp.arange(row_extent, dtype=jnp.int32)
    col_ids = col_first + jnp.arange(col_extent, dtype=jnp.int32)
    row_inside = (row_ids >= 0) & (row_ids < bins_side)
    col_inside = (col_ids >= 0) & (col_ids < bins_side)
    return (row_inside[:, None] & col_inside[None, :])[None]


def direct_move(source, axis_dim, extent, position, offset, sender):
    length = source.shape[axis_dim]
    layout = source.shape[:axis_dim] + (2, length // 2) + source.shape[axis_dim + 1 :]
    halves = jnp.moveaxis(source.reshape(layout), axis_dim, 0)
    targets = jnp.arange(extent, dtype=jnp.int32)
    owners = offset + targets // 2
    chosen = jnp.take(halves, targets % 2, axis=0)
    keeping = (owners == position).reshape((extent,) + (1,) * source.ndim)
    outgoing = jnp.where(keeping, chosen, jnp.zeros_like(chosen))
    incoming = sender(outgoing)
    return lax.dynamic_index_in_dim(incoming, offset + position // 2, 0, keepdims=False)


def per_device(
    coarse_feats,
    fine_feats,
    pair_prior,
    zoom_start,
    coarse_weights,
    coarse_bias,
    refine_first,
    refine_second,
    refine_bias,
):
    channels, tile_rows, tile_cols = pair_prior.shape
    row_count = lax.axis_size("row")
    col_count = lax.axis_size("col")
    bins_side = tile_rows * row_count
    row_place = lax.axis_index("row")
    col_place = lax.axis_index("col")
    row_start = row_place * tile_rows
    col_start = col_place * tile_cols
    coarse_all, fine_all = (
        lax.all_gather(coarse_feats, ("row", "col"), axis=1, tiled=True),
        lax.all_gather(fine_feats, ("row", "col"), axis=1, tiled=True),
    )
    coarse_padded = jnp.pad(coarse_all, ((0, 0), (margin_bins, margin_bins)))
    fine_padded = jnp.pad(fine_all, ((0, 0), (margin_bins, margin_bins)))
    pair_map = (
        pair_sum(coarse_padded, row_start, col_start, tile_rows, tile_cols)
        + pair_prior.astype(jnp.float32)
    ).astype(jnp.bfloat16)
    padded = with_halo(pair_map, (("row", 1), ("col", 2)), 2)
    hidden_coarse = conv_layer(
        padded, coarse_weights[0], coarse_bias[0], 2, tile_rows, tile_cols
    ).astype(jnp.bfloat16)
    padded = with_halo(hidden_coarse, (("row", 1), ("col", 2)), 4)
    coarse_map = conv_layer(
        padded, coarse_weights[1], coarse_bias[1], 4, tile_rows, tile_cols
    ).astype(jnp.bfloat16)
    zoom_bin = zoom_start[0]
    col_offset = zoom_bin // tile_cols
    row_offset = zoom_bin // tile_rows
    narrowed = direct_move(
        coarse_map,
        2,
        col_count,
        col_place,
        col_offset,
        lambda outgoing: lax.all_to_all(outgoing, "col", split_axis=0, concat_axis=0, tiled=True),
    )
    window = direct_move(
        narrowed,
        1,
        row_count,
        row_place,
        row_offset,
        lambda outgoing: lax.all_to_all(outgoing, "row", split_axis=0, concat_axis=0, tiled=True),
    )
    upsampled = jnp.broadcast_to(
        window[:, :, None, :, None], (channels, tile_rows // 2, 2, tile_cols // 2, 2)
    ).reshape(channels, tile_rows, tile_cols)
    window_padded = with_halo(upsampled, (("row", 1), ("col", 2)), 8)
    inside = inside_grid(row_start - 8, col_start - 8, tile_rows + 16, tile_cols + 16, bins_side)
    fine_pair = jnp.where(
        inside,
        pair_sum(fine_padded, row_start - 8, col_start - 8, tile_rows + 16, tile_cols + 16),
        0.0,
    ).astype(jnp.bfloat16)
    joined = jnp.concatenate([window_padded, fine_pair], axis=0)
    hidden_refine = conv_layer(
        joined, refine_first, refine_bias[0], 8, tile_rows, tile_cols
    ).astype(jnp.bfloat16)
    padded = with_halo(hidden_refine, (("row", 1), ("col", 2)), 16)
    refined = conv_layer(padded, refine_second, refine_bias[1], 16, tile_rows, tile_cols).astype(
        jnp.bfloat16
    )
    return (coarse_map, refined)


def solution(mesh):
    return jax.shard_map(
        per_device,
        mesh=mesh,
        in_specs=(
            P(None, ("row", "col")),
            P(None, ("row", "col")),
            P(None, "row", "col"),
            P(),
            P(),
            P(),
            P(),
            P(),
            P(),
        ),
        out_specs=(P(None, "row", "col"), P(None, "row", "col")),
        check_vma=False,
    )
```

profile of v0, /device:TPU:10, one launch (start us, length us, event | category | flops | bytes accessed | tf_op | source)
XLA Modules:
  0.0 436.0 jit_solution(9196025659374273345)
XLA Ops:
  0.6 58.1 %all_gather.6 = bf16[64,512]{0,1:T(8,128)(2,1)S(1)} all-gather(bf16[64,16]{0,1:T(8,128)(2,1)} %param.9), channel_id=1, replica_groups=mesh['row'=8,'col'=4] {'row','col'}, dimensions={1}, use_global_device_ids=true | all-gather | bytes 67584 | tf_op jit(solution)/shard_map/all_gather | solution.py:101
  59.1 2.0 add_convert_fusion
  61.2 3.2 collective-permute-start.1
  64.4 3.1 collective-permute-start
  68.3 5.9 %collective-permute-done = bf16[64,2,128]{2,0,1:T(8,128)(2,1)S(1)} collective-permute-done((bf16[64,2,128]{2,0,1:T(8,128)(2,1)S(1)}, bf16[64,2,128]{2,0,1:T(8,128)(2,1)S(1)}, u32[]{:S(2)}, u32[]{:S(2)}) %collective-permute-start) | collective-permute-done | bytes 32800 | tf_op jit(solution)/shard_map/ppermute | solution.py:14
  74.8 1.4 copy.137
  76.2 4.0 collective-permute-start.2
  80.2 1.4 copy.139
  81.6 4.2 collective-permute-start.3
  86.1 1.9 copy.138
  88.0 1.9 copy.140
  90.0 2.2 maximum_maximum_fusion.2
  92.2 1.7 fusion.100
  93.9 8.5 %fusion.37 = (bf16[64,24,8,128]{3,2,1,0:T(8,128)(2,1)S(1)}, bf16[64,24,8,128]{3,2,1,0:T(8,128)(2,1)S(1)}, bf16[64,24,8,128]{3,2,1,0:T(8,128)(2,1)S(1)}) fusion(bf16[64,2,128]{2,0,1:T(8,128)(2,1)S(1)} %collective-permute-done.1, bf16[64,64,128]{2,0,1:T(8,128)(2,1)S(1)} %add_convert_fusion, bf16[64,64,128]{2,0,1:T(8,128)(2,1)S(1)} %get-tuple-element.83, ...), kind=kLoop, calls=%fused_computation.62 | loop fusion | flops 34603008 | bytes 16842752
  105.0 1.9 collective-permute-start.5
  107.0 2.4 collective-permute-start.4
  109.4 3.1 collective-permute-done.4
  113.2 2.0 copy.145
  115.3 2.3 collective-permute-start.6
  119.0 3.9 collective-permute-start.7
  122.9 2.0 copy.146
  125.7 2.9 copy.148
  128.5 2.3 maximum_maximum_fusion.1
  132.6 9.4 %fusion.31 = (bf16[64,24,8,128]{3,2,1,0:T(8,128)(2,1)S(1)}, bf16[64,24,8,128]{3,2,1,0:T(8,128)(2,1)S(1)}, bf16[64,24,8,128]{3,2,1,0:T(8,128)(2,1)S(1)}) fusion(bf16[64,4,128]{2,0,1:T(8,128)(2,1)S(1)} %collective-permute-done.5, bf16[64,64,128]{2,0,1:T(8,128)(2,1)S(1)} %fusion.49, bf16[64,64,128]{2,0,1:T(8,128)(2,1)S(1)} %get-tuple-element.32, ...), kind=kLoop, calls=%fused_computation.54 | loop fusion | flops 34603008 | bytes 16908288
  144.2 4.4 %reshape.256 = f32[64,64,2,64]{3,2,1,0:T(2,128)} reshape(f32[64,8192]{1,0:T(8,128)S(1)} %bitcast.163) | data formatting | bytes 4194304 | tf_op jit(solution)/shard_map/reshape | solution.py:42
  148.6 4.1 fusion.41
  152.7 4.7 %gather_fusion = bf16[4,64,64,64]{3,2,1,0:T(8,128)(2,1)} fusion(bf16[2,64,64,64]{3,2,1,0:T(8,128)(2,1)} %fusion.41, s32[1024]{0:T(1024)S(1)} %pad_clamp_fusion.1), kind=kCustom, calls=%fused_computation | custom fusion | bytes 4194320 | tf_op jit(solution)/shard_map/jit(_take)/gather | solution.py:74
  157.4 4.7 %select_select_fusion.1 = bf16[4,64,64,64]{3,2,1,0:T(8,128)(2,1)} fusion(bf16[4,64,64,64]{3,2,1,0:T(8,128)(2,1)} %gather_fusion, pred[4]{0:T(512)(128)(4,1)S(1)} %get-tuple-element.77, pred[4]{0:T(512)(128)(4,1)S(1)} %get-tuple-element.78), kind=kLoop, calls=%fused_computation.21 | loop fusion | flops 2097152 | bytes 4194312 | tf_op jit(solution)/shard_map/jit(_where)/select_n | solution.py:76
  162.0 5.9 %reshape.289 = bf16[4,2,131072]{2,1,0:T(2,128)(2,1)} reshape(bf16[4,64,64,64]{3,2,1,0:T(8,128)(2,1)} %select_select_fusion.1) | data formatting | bytes 4194304
  168.0 6.2 %all-to-all-start = ((bf16[4,2,131072]{2,1,0:T(2,128)(2,1)}), bf16[4,2,131072]{2,1,0:T(2,128)(2,1)}, u32[]{:S(2)}, u32[]{:S(2)}) async-start(bf16[4,2,131072]{2,1,0:T(2,128)(2,1)} %reshape.289), calls=%async_computation | async-start | bytes 4194304 | tf_op jit(solution)/shard_map/all_to_all | solution.py:127
  174.3 44.1 %all-to-all-done = bf16[4,2,131072]{2,1,0:T(2,128)(2,1)} async-done(((bf16[4,2,131072]{2,1,0:T(2,128)(2,1)}), bf16[4,2,131072]{2,1,0:T(2,128)(2,1)}, u32[]{:S(2)}, u32[]{:S(2)}) %all-to-all-start) | async-done | bytes 2097184 | tf_op jit(solution)/shard_map/all_to_all | solution.py:127
  218.3 5.8 %reshape.290 = bf16[4,64,64,64]{3,2,1,0:T(8,128)(2,1)} reshape(bf16[4,2,131072]{2,1,0:T(2,128)(2,1)} %all-to-all-done) | data formatting | bytes 4194304
  225.4 3.1 gather_fusion.1
  228.5 4.7 %select_select_fusion = bf16[8,64,32,64]{3,2,1,0:T(8,128)(2,1)} fusion(bf16[8,64,32,64]{3,2,1,0:T(8,128)(2,1)} %gather_fusion.1, pred[8]{0:T(512)(128)(4,1)S(1)} %get-tuple-element.79, pred[8]{0:T(512)(128)(4,1)S(1)} %get-tuple-element.80), kind=kLoop, calls=%fused_computation.20 | loop fusion | flops 2097152 | bytes 4194320 | tf_op jit(solution)/shard_map/jit(_where)/select_n | solution.py:76
  233.2 7.6 %reshape.291 = bf16[8,2,65536]{2,1,0:T(2,128)(2,1)} reshape(bf16[8,64,32,64]{3,2,1,0:T(8,128)(2,1)} %select_select_fusion) | data formatting | bytes 4194304
  240.8 4.4 %all-to-all-start.1 = ((bf16[8,2,65536]{2,1,0:T(2,128)(2,1)}), bf16[8,2,65536]{2,1,0:T(2,128)(2,1)}, u32[]{:S(2)}, u32[]{:S(2)}) async-start(bf16[8,2,65536]{2,1,0:T(2,128)(2,1)} %reshape.291), calls=%async_computation.1 | async-start | bytes 4194304 | tf_op jit(solution)/shard_map/all_to_all | solution.py:135
  245.2 61.3 %all_gather.7 = bf16[64,512]{0,1:T(8,128)(2,1)S(1)} all-gather(bf16[64,16]{0,1:T(8,128)(2,1)S(1)} %copy-done.12), channel_id=1, replica_groups=mesh['row'=8,'col'=4] {'row','col'}, dimensions={1}, use_global_device_ids=true | all-gather | bytes 67584 | tf_op jit(solution)/shard_map/all_gather | solution.py:102
  306.7 4.5 %select_convert_fusion = bf16[64,80,144]{0,2,1:T(8,128)(2,1)} fusion(f32[64,144]{0,1:T(8,128)S(1)} %fusion.57, f32[64,80]{0,1:T(8,128)S(1)} %fusion.76, pred[80,144]{1,0:T(8,128)(4,1)S(1)} %broadcast_and_fusion), kind=kLoop, calls=%fused_computation.16 | loop fusion | flops 2211840 | bytes 1543424 | tf_op jit(solution)/shard_map/convert_element_type | solution.py:146
  311.2 7.4 %reshape.292 = bf16[8,64,32,64]{3,2,1,0:T(8,128)(2,1)} reshape(bf16[8,2,65536]{2,1,0:T(2,128)(2,1)} %all-to-all-done.1) | data formatting | bytes 4194304
  320.3 2.0 broadcast_in_dim.78
  322.4 2.6 collective-permute-start.9
  325.0 1.9 collective-permute-start.8
  327.0 1.9 collective-permute-done.9
  328.9 8.3 %collective-permute-done.8 = bf16[64,8,128]{0,2,1:T(8,128)(2,1)S(1)} collective-permute-done((bf16[64,8,128]{0,2,1:T(8,128)(2,1)S(1)}, bf16[64,8,128]{0,2,1:T(8,128)(2,1)S(1)}, u32[]{:S(2)}, u32[]{:S(2)}) %collective-permute-start.8) | collective-permute-done | bytes 131104 | tf_op jit(solution)/shard_map/ppermute | solution.py:14
  337.2 5.1 %collective-permute-start.11 = (bf16[64,80,8]{0,2,1:T(8,128)(2,1)S(1)}, bf16[64,80,8]{0,2,1:T(8,128)(2,1)S(1)}, u32[]{:S(2)}, u32[]{:S(2)}) collective-permute-start(bf16[64,80,8]{0,2,1:T(8,128)(2,1)S(1)} %get-tuple-element.28), channel_id=1, source_target_pairs={{1,0},{2,1},{3,2},{5,4},{6,5},{7,6},{9,8},{10,9},{11,10},{13,12},{... | collective-permute-start | bytes 245768 | tf_op jit(solution)/shard_map/ppermute | solution.py:17
  342.3 1.9 collective-permute-start.10
  344.3 1.6 collective-permute-done.11
  345.8 3.7 collective-permute-done.10
  349.5 3.7 pad_maximum_fusion.7
  353.2 5.1 %fusion.97 = (bf16[128,64,128]{0,2,1:T(8,128)(2,1)S(1)}, bf16[128,64,128]{0,2,1:T(8,128)(2,1)S(1)}, bf16[128,64,128]{0,2,1:T(8,128)(2,1)S(1)}, bf16[128,64,128]{...) fusion(bf16[128,80,144]{0,2,1:T(8,128)(2,1)S(1)} %pad_maximum_f, ...), kind=kLoop, calls=%fused_computation.176 | loop fusion | bytes 37748736 | tf_op jit(solution)/shard_map/slice | solution.py:29
  370.3 1.9 collective-permute-start.13
  372.5 2.4 collective-permute-start.12
  376.2 3.9 collective-permute-done.12
  381.1 2.3 fusion.103
  383.4 3.3 copy.160
  386.7 2.0 collective-permute-start.14
  388.7 3.3 copy.163
  392.0 4.7 %collective-permute-start.15 = (bf16[64,96,16]{1,2,0:T(8,128)(2,1)}, bf16[64,96,16]{1,2,0:T(8,128)(2,1)}, u32[]{:S(2)}, u32[]{:S(2)}) collective-permute-start(bf16[64,96,16]{1,2,0:T(8,128)(2,1)} %copy.163), channel_id=1, source_target_pairs={{1,0},{2,1},{3,2},{5,4},{6,5},{7,6},{9,8},{10,9},{11,10},{13,12},{... | collective-permute-start | bytes 589832 | tf_op jit(solution)/shard_map/ppermute | solution.py:17
  397.1 1.6 copy.170
  398.8 3.1 copy.161
  402.5 3.9 copy.164
  406.4 7.9 %maximum_maximum_fusion = (bf16[64,96,144]{2,0,1:T(8,128)(2,1)S(1)}, bf16[64,96,144]{2,0,1:T(8,128)(2,1)S(1)}) fusion(bf16[64,16,128]{2,0,1:T(8,128)(2,1)S(1)} %copy.159, bf16[64,64,128]{2,0,1:T(8,128)(2,1)S(1)} %fusion.45, bf16[64,16,128]{2,0,1:T(8,128)(2,1)S(1)} %copy-done.7, bf16[64,96,16]{2,0,1:T(8,128)(2,1)S(1)} %copy.161, bf16[64,96,16]{2,0,1:T(8,128)(2,1)} %copy.164), kind=kLoop, calls=%fused_computation.69 | loop fusion | flops 14155776 | bytes 5505024 | tf_op jit(solution)/shard_map/concatenate | solution.py:18
  416.1 15.3 %fusion.25 = (bf16[64,24,8,128]{3,2,1,0:T(8,128)(2,1)S(1)}, bf16[64,24,8,128]{3,2,1,0:T(8,128)(2,1)S(1)}, bf16[64,24,8,128]{3,2,1,0:T(8,128)(2,1)S(1)}) fusion(bf16[64,16,128]{2,0,1:T(8,128)(2,1)S(1)} %copy.159, bf16[64,64,128]{2,0,1:T(8,128)(2,1)S(1)} %fusion.45, bf16[64,64,128]{2,0,1:T(8,128)(2,1)S(1)} %get-tuple-element.15, ...), kind=kLoop, calls=%fused_computation.46 | loop fusion | flops 34603008 | bytes 17301504
  434.1 1.6 copy.171
  (102 shorter events, 34.2 us)
Async XLA Ops:
  61.2 7.1 %collective-permute-start.1 = (bf16[64,2,128]{2,0,1:T(8,128)(2,1)S(1)}, bf16[64,2,128]{2,0,1:T(8,128)(2,1)S(1)}, u32[]{:S(2)}, u32[]{:S(2)}) collective-permute-start(bf16[64,2,128]{2,0,1:T(8,128)(2,1)S(1)} %get-tuple-element.68), channel_id=1, source_target_pairs={{4,0},{8,4},{12,8},{16,12},{20,16},{24,20},{28,24},{5,1},{9,5},{13... | collective-permute-start | bytes 98312 | tf_op jit(solution)/shard_map/ppermute | solution.py:17
  64.4 9.7 %collective-permute-start = (bf16[64,2,128]{2,0,1:T(8,128)(2,1)S(1)}, bf16[64,2,128]{2,0,1:T(8,128)(2,1)S(1)}, u32[]{:S(2)}, u32[]{:S(2)}) collective-permute-start(bf16[64,2,128]{2,0,1:T(8,128)(2,1)S(1)} %get-tuple-element.69), channel_id=1, source_target_pairs={{0,4},{4,8},{8,12},{12,16},{16,20},{20,24},{24,28},{1,5},{5,9},{9,... | collective-permute-start | bytes 98312 | tf_op jit(solution)/shard_map/ppermute | solution.py:14
  74.3 11.6 %copy-start.14 = (s32[2]{0:T(128)S(1)}, s32[2]{0:T(128)}, u32[]{:S(2)}) copy-start(s32[2]{0:T(128)} %param.12) | copy-start | bytes 28
  76.2 9.9 %collective-permute-start.2 = (bf16[64,68,2]{1,0,2:T(8,128)(2,1)S(1)}, bf16[64,68,2]{1,0,2:T(8,128)(2,1)S(1)}, u32[]{:S(2)}, u32[]{:S(2)}) collective-permute-start(bf16[64,68,2]{1,0,2:T(8,128)(2,1)S(1)} %copy.137), channel_id=1, source_target_pairs={{0,1},{1,2},{2,3},{4,5},{5,6},{6,7},{8,9},{9,10},{10,11},{12,13},{... | collective-permute-start | bytes 52232 | tf_op jit(solution)/shard_map/ppermute | solution.py:14
  81.6 6.4 %collective-permute-start.3 = (bf16[64,68,2]{1,0,2:T(8,128)(2,1)S(1)}, bf16[64,68,2]{1,0,2:T(8,128)(2,1)S(1)}, u32[]{:S(2)}, u32[]{:S(2)}) collective-permute-start(bf16[64,68,2]{1,0,2:T(8,128)(2,1)S(1)} %copy.139), channel_id=1, source_target_pairs={{1,0},{2,1},{3,2},{5,4},{6,5},{7,6},{9,8},{10,9},{11,10},{13,12},{... | collective-permute-start | bytes 52232 | tf_op jit(solution)/shard_map/ppermute | solution.py:17
  93.9 8.5 %copy-start.8 = (bf16[2,3,64,192]{3,2,1,0:T(8,128)(2,1)S(1)}, bf16[2,3,64,192]{3,2,1,0:T(8,128)(2,1)}, u32[]{:S(2)}) copy-start(bf16[2,3,64,192]{3,2,1,0:T(8,128)(2,1)} %param.13) | copy-start | bytes 442372
  105.0 4.4 collective-permute-start.5
  107.0 5.6 %collective-permute-start.4 = (bf16[64,4,128]{2,0,1:T(8,128)(2,1)S(1)}, bf16[64,4,128]{2,0,1:T(8,128)(2,1)S(1)}, u32[]{:S(2)}, u32[]{:S(2)}) collective-permute-start(bf16[64,4,128]{2,0,1:T(8,128)(2,1)S(1)} %get-tuple-element.64), channel_id=1, source_target_pairs={{0,4},{4,8},{8,12},{12,16},{16,20},{20,24},{24,28},{1,5},{5,9},{9,... | collective-permute-start | bytes 196616 | tf_op jit(solution)/shard_map/ppermute | solution.py:14
  115.3 7.7 %collective-permute-start.6 = (bf16[64,72,4]{1,0,2:T(8,128)(2,1)}, bf16[64,72,4]{1,0,2:T(8,128)(2,1)S(1)}, u32[]{:S(2)}, u32[]{:S(2)}) collective-permute-start(bf16[64,72,4]{1,0,2:T(8,128)(2,1)} %copy.145), channel_id=1, source_target_pairs={{0,1},{1,2},{2,3},{4,5},{5,6},{6,7},{8,9},{9,10},{10,11},{12,13},{... | collective-permute-start | bytes 110600 | tf_op jit(solution)/shard_map/ppermute | solution.py:14
  119.0 6.7 %collective-permute-start.7 = (bf16[64,72,4]{1,0,2:T(8,128)(2,1)S(1)}, bf16[64,72,4]{1,0,2:T(8,128)(2,1)}, u32[]{:S(2)}, u32[]{:S(2)}) collective-permute-start(bf16[64,72,4]{1,0,2:T(8,128)(2,1)S(1)} %copy.147), channel_id=1, source_target_pairs={{1,0},{2,1},{3,2},{5,4},{6,5},{7,6},{9,8},{10,9},{11,10},{13,12},{... | collective-permute-start | bytes 110600 | tf_op jit(solution)/shard_map/ppermute | solution.py:17
  132.6 9.4 %copy-start.9 = (bf16[2,3,64,192]{3,2,1,0:T(8,128)(2,1)S(1)}, bf16[2,3,64,192]{3,2,1,0:T(8,128)(2,1)}, u32[]{:S(2)}) copy-start(bf16[2,3,64,192]{3,2,1,0:T(8,128)(2,1)} %param.13) | copy-start | bytes 442372
  168.0 50.4 %all-to-all-start = ((bf16[4,2,131072]{2,1,0:T(2,128)(2,1)}), bf16[4,2,131072]{2,1,0:T(2,128)(2,1)}, u32[]{:S(2)}, u32[]{:S(2)}) async-start(bf16[4,2,131072]{2,1,0:T(2,128)(2,1)} %reshape.289), calls=%async_computation | async-start | bytes 4194304 | tf_op jit(solution)/shard_map/all_to_all | solution.py:127
  240.8 4.5 %copy-start.12 = (bf16[64,16]{0,1:T(8,128)(2,1)S(1)}, bf16[64,16]{0,1:T(8,128)(2,1)}, u32[]{:S(2)}) copy-start(bf16[64,16]{0,1:T(8,128)(2,1)} %param.10) | copy-start | bytes 6148
  240.8 70.4 %all-to-all-start.1 = ((bf16[8,2,65536]{2,1,0:T(2,128)(2,1)}), bf16[8,2,65536]{2,1,0:T(2,128)(2,1)}, u32[]{:S(2)}, u32[]{:S(2)}) async-start(bf16[8,2,65536]{2,1,0:T(2,128)(2,1)} %reshape.291), calls=%async_computation.1 | async-start | bytes 4194304 | tf_op jit(solution)/shard_map/all_to_all | solution.py:135
  318.6 8.3 %copy-start.10 = (bf16[3,64,384]{2,1,0:T(8,128)(2,1)S(1)}, bf16[3,64,384]{2,1,0:T(8,128)(2,1)}, u32[]{:S(2)}) copy-start(bf16[3,64,384]{2,1,0:T(8,128)(2,1)} %param.15) | copy-start | bytes 442372
  320.3 23.9 %copy-start.13 = (f32[2,64]{1,0:T(2,128)S(1)}, f32[2,64]{1,0:T(2,128)}, u32[]{:S(2)}) copy-start(f32[2,64]{1,0:T(2,128)} %param.17) | copy-start | bytes 1540
  320.3 29.2 %copy-start = (bf16[64,80,144]{0,2,1:T(8,128)(2,1)S(1)}, bf16[64,80,144]{0,2,1:T(8,128)(2,1)}, u32[]{:S(2)}) copy-start(bf16[64,80,144]{0,2,1:T(8,128)(2,1)} %select_convert_fusion) | copy-start | bytes 4423684
  322.4 6.5 %collective-permute-start.9 = (bf16[64,8,128]{0,2,1:T(8,128)(2,1)S(1)}, bf16[64,8,128]{0,2,1:T(8,128)(2,1)S(1)}, u32[]{:S(2)}, u32[]{:S(2)}) collective-permute-start(bf16[64,8,128]{0,2,1:T(8,128)(2,1)S(1)} %get-tuple-element.42), channel_id=1, source_target_pairs={{4,0},{8,4},{12,8},{16,12},{20,16},{24,20},{28,24},{5,1},{9,5},{13... | collective-permute-start | bytes 393224 | tf_op jit(solution)/shard_map/ppermute | solution.py:17
  325.0 12.2 %collective-permute-start.8 = (bf16[64,8,128]{0,2,1:T(8,128)(2,1)S(1)}, bf16[64,8,128]{0,2,1:T(8,128)(2,1)S(1)}, u32[]{:S(2)}, u32[]{:S(2)}) collective-permute-start(bf16[64,8,128]{0,2,1:T(8,128)(2,1)S(1)} %get-tuple-element.41), channel_id=1, source_target_pairs={{0,4},{4,8},{8,12},{12,16},{16,20},{20,24},{24,28},{1,5},{5,9},{9,... | collective-permute-start | bytes 393224 | tf_op jit(solution)/shard_map/ppermute | solution.py:14
  337.2 8.6 %collective-permute-start.11 = (bf16[64,80,8]{0,2,1:T(8,128)(2,1)S(1)}, bf16[64,80,8]{0,2,1:T(8,128)(2,1)S(1)}, u32[]{:S(2)}, u32[]{:S(2)}) collective-permute-start(bf16[64,80,8]{0,2,1:T(8,128)(2,1)S(1)} %get-tuple-element.28), channel_id=1, source_target_pairs={{1,0},{2,1},{3,2},{5,4},{6,5},{7,6},{9,8},{10,9},{11,10},{13,12},{... | collective-permute-start | bytes 245768 | tf_op jit(solution)/shard_map/ppermute | solution.py:17
  342.3 7.2 %collective-permute-start.10 = (bf16[64,80,8]{0,2,1:T(8,128)(2,1)S(1)}, bf16[64,80,8]{0,2,1:T(8,128)(2,1)S(1)}, u32[]{:S(2)}, u32[]{:S(2)}) collective-permute-start(bf16[64,80,8]{0,2,1:T(8,128)(2,1)S(1)} %get-tuple-element.27), channel_id=1, source_target_pairs={{0,1},{1,2},{2,3},{4,5},{5,6},{6,7},{8,9},{9,10},{10,11},{12,13},{... | collective-permute-start | bytes 245768 | tf_op jit(solution)/shard_map/ppermute | solution.py:14
  358.4 1.6 copy-start.5
  360.0 1.6 copy-start.4
  361.5 1.6 copy-start.3
  363.1 1.6 copy-start.2
  364.7 1.6 copy-start.1
  370.3 5.8 %collective-permute-start.13 = (bf16[64,16,128]{2,1,0:T(8,128)(2,1)S(1)}, bf16[64,16,128]{2,1,0:T(8,128)(2,1)S(1)}, u32[]{:S(2)}, u32[]{:S(2)}) collective-permute-start(bf16[64,16,128]{2,1,0:T(8,128)(2,1)S(1)} %copy.157), channel_id=1, source_target_pairs={{4,0},{8,4},{12,8},{16,12},{20,16},{24,20},{28,24},{5,1},{9,5},{13... | collective-permute-start | bytes 786440 | tf_op jit(solution)/shard_map/ppermute | solution.py:17
  372.5 7.7 %collective-permute-start.12 = (bf16[64,16,128]{2,1,0:T(8,128)(2,1)S(1)}, bf16[64,16,128]{2,1,0:T(8,128)(2,1)S(1)}, u32[]{:S(2)}, u32[]{:S(2)}) collective-permute-start(bf16[64,16,128]{2,1,0:T(8,128)(2,1)S(1)} %copy.156), channel_id=1, source_target_pairs={{0,4},{4,8},{8,12},{12,16},{16,20},{20,24},{24,28},{1,5},{5,9},{9,... | collective-permute-start | bytes 786440 | tf_op jit(solution)/shard_map/ppermute | solution.py:14
  380.2 0.7 copy-start.6
  386.7 12.1 %collective-permute-start.14 = (bf16[64,96,16]{1,2,0:T(8,128)(2,1)}, bf16[64,96,16]{1,2,0:T(8,128)(2,1)}, u32[]{:S(2)}, u32[]{:S(2)}) collective-permute-start(bf16[64,96,16]{1,2,0:T(8,128)(2,1)} %copy.160), channel_id=1, source_target_pairs={{0,1},{1,2},{2,3},{4,5},{5,6},{6,7},{8,9},{9,10},{10,11},{12,13},{... | collective-permute-start | bytes 589832 | tf_op jit(solution)/shard_map/ppermute | solution.py:14
  392.0 10.5 %collective-permute-start.15 = (bf16[64,96,16]{1,2,0:T(8,128)(2,1)}, bf16[64,96,16]{1,2,0:T(8,128)(2,1)}, u32[]{:S(2)}, u32[]{:S(2)}) collective-permute-start(bf16[64,96,16]{1,2,0:T(8,128)(2,1)} %copy.163), channel_id=1, source_target_pairs={{1,0},{2,1},{3,2},{5,4},{6,5},{7,6},{9,8},{10,9},{11,10},{13,12},{... | collective-permute-start | bytes 589832 | tf_op jit(solution)/shard_map/ppermute | solution.py:17
  397.1 9.3 %copy-start.7 = (bf16[64,16,128]{2,0,1:T(8,128)(2,1)S(1)}, bf16[64,16,128]{2,0,1:T(8,128)(2,1)}, u32[]{:S(2)}) copy-start(bf16[64,16,128]{2,0,1:T(8,128)(2,1)} %copy-done.6) | copy-start | bytes 786436
  416.1 15.4 %copy-start.11 = (bf16[3,64,192]{2,1,0:T(8,128)(2,1)S(1)}, bf16[3,64,192]{2,1,0:T(8,128)(2,1)}, u32[]{:S(2)}) copy-start(bf16[3,64,192]{2,1,0:T(8,128)(2,1)} %param.16) | copy-start | bytes 221188
where the time goes:
time: 443 us; the launch traced here: 436 us
  blocking collectives  119 us (27%)
  local copies, waits for them, and re-layouts  95.4 us (22%)
  waiting for transfers between devices  75.1 us (17%)
  other arithmetic  71.7 us (16%)
  starting transfers between devices  58.3 us (13%)
  matrix products  14.3 us (3%)
    all_gather x1, blocking collectives, per_device(): lax.all_gather(fine_feats, ('row', 'col'), axis=1, tiled=True)  61.3 us
    all_gather x1, blocking collectives, per_device(): lax.all_gather(coarse_feats, ('row', 'col'), axis=1, tiled=True)  58.1 us
    all_to_all x1, waiting for transfers between devices, per_device(): lax.all_to_all(outgoing, 'col', split_axis=0, concat_axis=0, tiled=True)  44.1 us
    unnamed x36, local copies, waits for them, and re-layouts  34.4 us
    unnamed x3, other arithmetic  33.3 us
    ppermute x8, starting transfers between devices, with_halo(): lax.ppermute(lax.slice_in_dim(block, 0, width, axis=dim), axis, backward)  27.6 us
    ppermute x8, waiting for transfers between devices, with_halo(): lax.ppermute(lax.slice_in_dim(block, block.shape[dim] - width, None, axis...  25 us
    ppermute x8, starting transfers between devices, with_halo(): lax.ppermute(lax.slice_in_dim(block, block.shape[dim] - width, None, axis...  20.1 us
  transfers between devices with their start and end apart: 18, of which 11 were waited for; matrix products, arithmetic and copies ran while one was open for 5% of the time, Pallas kernels for 0%

commit v1 on v0

v1 whole, which is shorter than its diff:
```python
import jax
import jax.numpy as jnp
from jax import lax
from jax.experimental import pallas as pl
from jax.experimental.pallas import tpu as pltpu
from jax.sharding import PartitionSpec as P

f32 = jnp.float32
bf16 = jnp.bfloat16
VMEM = pl.BlockSpec(memory_space=pltpu.VMEM)
SMEM = pl.BlockSpec(memory_space=pltpu.SMEM)


def call(body, outs, scratch, cost, name):
    flops, moved = cost
    def run(*args):
        return pl.pallas_call(
            body,
            out_shape=outs,
            in_specs=[SMEM] + [VMEM] * (len(args) - 1),
            out_specs=jax.tree.map(lambda _: VMEM, outs),
            scratch_shapes=scratch,
            compiler_params=pltpu.CompilerParams(vmem_limit_bytes=56 << 20),
            cost_estimate=pl.CostEstimate(flops=flops, bytes_accessed=moved, transcendentals=0),
            name=name,
        )(*args)

    return run


def roll(x, shift):
    shift = shift % x.shape[-1]
    return x if shift == 0 else pltpu.roll(x, shift, x.ndim - 1)


def lanes(shape):
    return lax.broadcasted_iota(jnp.int32, shape, len(shape) - 1)


def swap_pairs(count):
    first = [(i, i ^ 1) for i in range(count)]
    second = [(i, i + 1) for i in range(1, count - 1, 2)]
    return first, second + [(b, a) for a, b in second]


def dot(a, b):
    return jnp.dot(a, b, preferred_element_type=f32)


def pick_bins(feats, start, step):
    bins = feats.shape[0]
    shape = (bins, 128)
    hit = lax.broadcasted_iota(jnp.int32, shape, 0) == start + step * lanes(shape)
    return lax.dot_general(
        feats, hit.astype(f32).astype(bf16), (((0,), (0,)), ((), ())), preferred_element_type=f32
    )


def inside(start, step, bins, shape=(1, 128)):
    at = start + step * lanes(shape)
    return ((at >= 0) & (at < bins)).astype(f32)


def scalar_inside(at, bins):
    return ((at >= 0) & (at < bins)).astype(f32)


def strip_pack_tile(pos, center, row_a, row_b, out_a, out_b):
    rim = row_a.shape[0]
    rows = center.shape[0]
    odd_row = pos[0] % 2 == 1
    odd_col = pos[1] % 2 == 1
    lane = lanes(row_a.shape[1:]) // 8
    total = rows + 2 * rim
    for group in range(out_a.shape[0]):
        packed_a = jnp.zeros(row_a.shape[1:], f32)
        packed_b = packed_a
        for k in range(16):
            e = group * 16 + k
            if e >= total:
                break
            if e < rim:
                x = jnp.where(odd_row, row_a[e], row_b[e])
            elif e < rim + rows:
                x = center[e - rim]
            else:
                x = jnp.where(odd_row, row_b[e - rim - rows], row_a[e - rim - rows])
            x = x.astype(f32)
            turned = roll(x, 8)
            here = lane == k
            packed_a = jnp.where(here, roll(jnp.where(odd_col, x, turned), 8 * k), packed_a)
            packed_b = jnp.where(here, roll(jnp.where(odd_col, turned, x), 8 * k), packed_b)
        out_a[group] = packed_a.astype(bf16)
        out_b[group] = packed_b.astype(bf16)


def store_taps(ref, row, first, value, spacing):
    size = value.shape[0]
    for tap in range(3):
        ref[row, tap * size : (tap + 1) * size, first : first + 128] = roll(
            value, -spacing * tap
        ).astype(bf16)


def products(weights, taps, out, count):
    def one(row, carry):
        out[row] = dot(weights, taps[row])
        return carry

    lax.fori_loop(0, count, one, 0, unroll=4)


def combine(parts, row, spacing):
    size = parts.shape[1] // 3
    return (
        parts[row, :size]
        + parts[row + spacing, size : 2 * size]
        + parts[row + 2 * spacing, 2 * size :]
    )


def tile_kernel(
    pos, weights, bias, feats, center, row_a, row_b, col_a, col_b,
    coarse, m00, m01, m10, m11, s1, s2, parts, own_feats,
):
    rows, channels, width = center.shape
    half = width // 2
    rim = row_a.shape[0]
    bins = feats.shape[0]
    row_start = pos[0] * rows
    col_start = pos[1] * width
    odd_row = pos[0] % 2 == 1
    odd_col = pos[1] % 2 == 1
    all_feats = feats[...]
    own_feats[...] = pick_bins(all_feats, row_start - rim, 1)[:channels]
    col_feats = [
        pick_bins(all_feats, col_start + h * half - rim, 1)[:channels] for h in range(2)
    ]
    lane_in = [inside(col_start + h * half - rim, 1, bins) for h in range(2)]
    lane = lanes((channels, width))
    total = rows + 2 * rim
    for e in range(total):
        if e < rim:
            x = jnp.where(odd_row, row_a[e], row_b[e])
        elif e < rim + rows:
            x = center[e - rim]
        else:
            x = jnp.where(odd_row, row_b[e - rim - rows], row_a[e - rim - rows])
        x = x.astype(f32)
        group, k = divmod(e, 16)
        pa = col_a[group].astype(f32)
        pb = col_b[group].astype(f32)
        left = jnp.where(odd_col, pa, pb)
        right = jnp.where(odd_col, pb, pa)
        halves = (
            jnp.where(lane < rim, roll(left, -(8 * k + 8 - rim)), roll(x, rim)),
            jnp.where(lane < half + rim, roll(x, rim - half), roll(right, half + rim - 8 * k)),
        )
        ok = scalar_inside(row_start - rim + e, bins)
        own = own_feats[:, e : e + 1]
        for h in range(2):
            value = (halves[h] + (col_feats[h] + own)) * (lane_in[h] * ok)
            store_taps(s1, e, h * 128, value, 2)
    w1 = weights[0]
    b1 = bias[0]
    mask1 = jnp.concatenate(
        [inside(col_start + h * half - rim + 2, 1, bins) for h in range(2)], axis=1
    )

    products(w1, s1, parts, total)

    def first(e, carry):
        value = jnp.maximum(combine(parts, e, 2) + b1, 0.0)
        ok = scalar_inside(row_start - rim + 2 + e, bins)
        value = value * (mask1 * ok)
        for h in range(2):
            store_taps(s2, e, h * 128, value[:, h * 128 : h * 128 + 128], 4)
        return carry

    lax.fori_loop(0, total - 4, first, 0, unroll=4)
    w2 = weights[1]
    b2 = bias[1]

    products(w2, s2, parts, total - 4)
    low = lane < half
    messages = ((m00, m01), (m10, m11))
    upper = 2 * row_start < bins
    for u in range(2):

        def produce(p, carry, u=u):
            q = rows // 2 * u + 2 * p
            even = jnp.maximum(combine(parts, q, 4) + b2, 0.0)
            odd = jnp.maximum(combine(parts, q + 1, 4) + b2, 0.0)
            for t, value in ((0, even), (1, odd)):
                coarse[q + t] = jnp.where(
                    low, value[:, :128], roll(value[:, 128:], half)
                ).astype(bf16)
            sides = [
                jnp.where(
                    low,
                    even[:, v * 128 : v * 128 + 128],
                    roll(odd[:, v * 128 : v * 128 + 128], half),
                ).astype(bf16)
                for v in range(2)
            ]

            @pl.when(upper)
            def _():
                for v in range(2):
                    messages[u][v][p] = sides[v]

            @pl.when(jnp.logical_not(upper))
            def _():
                for v in range(2):
                    messages[1 - u][1 - v][p] = sides[v]

            return carry

        lax.fori_loop(0, rows // 4, produce, 0, unroll=4)


def strip_pack_window(pos, center, row_a, row_b, out_a, out_b):
    rim = row_a.shape[0]
    pairs = center.shape[0]
    odd_row = pos[0] % 2 == 1
    odd_col = pos[1] % 2 == 1
    slot = lanes(row_a.shape[1:]) % 64 // 16
    for group in range(out_a.shape[0]):
        packed_a = jnp.zeros(row_a.shape[1:], f32)
        packed_b = packed_a
        for m in range(4):
            g = group * 4 + m
            if g < rim:
                x = jnp.where(odd_row, row_a[g], row_b[g])
            elif g < rim + pairs:
                x = center[g - rim]
            else:
                x = jnp.where(odd_row, row_b[g - rim - pairs], row_a[g - rim - pairs])
            x = x.astype(f32)
            turned = roll(x, 80)
            here = slot == m
            packed_a = jnp.where(here, roll(jnp.where(odd_col, x, turned), 16 * m), packed_a)
            packed_b = jnp.where(here, roll(jnp.where(odd_col, turned, x), 16 * m), packed_b)
        out_a[group] = packed_a.astype(bf16)
        out_b[group] = packed_b.astype(bf16)


def fine_kernel(pos, row_weights, col_weights, bias, feats, row_terms, col_terms, parts):
    channels = bias.shape[0]
    bins = feats.shape[0]
    row_start = pos[0] * pos[2]
    col_start = pos[1] * pos[3]
    all_feats = feats[...]

    def stacked(start, step, shift):
        picked = pick_bins(all_feats, start, step)[channels:]
        taps = [roll(picked, -shift * tap) for tap in range(3)]
        return jnp.concatenate(taps, 0).astype(bf16)

    parts[...] = dot(row_weights[...], stacked(row_start - 24, 1, 8))
    at = col_start - 16 + 2 * lanes((1, 128))
    left_in = ((at >= 8) & (at < bins + 8)).astype(f32)
    right_in = ((at >= -8) & (at < bins - 8)).astype(f32)
    b = bias[...]
    for n in range(row_terms.shape[0]):
        row_terms[n] = (
            parts[channels : 2 * channels, n : n + 1]
            + b
            + parts[:channels, n : n + 1] * left_in
            + parts[2 * channels :, n : n + 1] * right_in
        )
    for v in range(2):
        terms = dot(col_weights[...], stacked(col_start - 24 + v, 2, 4))
        for a in range(3):
            col_terms[v, a] = terms[a * channels : (a + 1) * channels]


def refine_kernel(
    pos, weights, weights2, bias2, center, row_a, row_b, col_a, col_b, row_terms, col_terms,
    refined, sw, sh, products_w, products_h,
):
    pairs, channels, _ = center.shape
    rim = row_a.shape[0]
    rows, cols, bins = pos[2], pos[3], pos[4]
    row_start = pos[0] * rows
    col_start = pos[1] * cols
    odd_row = pos[0] % 2 == 1
    odd_col = pos[1] % 2 == 1
    lane = lanes((channels, 128))
    total = pairs + 2 * rim
    for g in range(total):
        if g < rim:
            x = jnp.where(odd_row, row_a[g], row_b[g])
        elif g < rim + pairs:
            x = center[g - rim]
        else:
            x = jnp.where(odd_row, row_b[g - rim - pairs], row_a[g - rim - pairs])
        x = x.astype(f32)
        group, m = divmod(g, 4)
        pa = col_a[group].astype(f32)
        pb = col_b[group].astype(f32)
        left = jnp.where(odd_col, pa, pb)
        right = jnp.where(odd_col, pb, pa)
        for t in range(2):
            base = 64 * t + 16 * m
            value = jnp.where(
                lane < 12,
                roll(left, -(base + 4)),
                jnp.where(lane < 76, roll(x, 12 - 64 * t), roll(right, 76 - base)),
            )
            store_taps(sw, g, t * 128, value, 4)
    w1 = weights[...]
    col_in = inside(col_start - 16, 2, bins)
    low = lane < 64

    products(w1, sw, products_w, total)

    def first(n, carry):
        both = combine(products_w, n, 2)
        for t in range(2):
            k = 2 * n + t
            base = both[:, t * 128 : t * 128 + 128]
            at = row_start - 16 + 2 * k
            above = scalar_inside(at - 8, bins)
            below = scalar_inside(at + 8, bins)
            mask = col_in * scalar_inside(at, bins)
            sums = [
                base + (col_terms[v, 1] + col_terms[v, 0] * above + col_terms[v, 2] * below)
                for v in range(2)
            ]
            for u in range(2):
                own = row_terms[2 * k + u]
                h = [jnp.maximum(s + own, 0.0) * mask for s in sums]
                for tap in range(3):
                    sh[k, tap * channels : (tap + 1) * channels, u * 128 : u * 128 + 128] = (
                        jnp.where(low, roll(h[0], -8 * tap), roll(h[1], 64 - 8 * tap)).astype(bf16)
                    )
        return carry

    inner = total - 4
    lax.fori_loop(0, inner, first, 0, unroll=2)
    w2 = weights2[...]
    b2 = bias2[...]

    products(w2, sh, products_h, sh.shape[0])
    source = lax.broadcasted_iota(jnp.int32, (128, 128), 0)
    spread = 2 * (source % 64) + source // 64 == lanes((128, 128))
    spread = spread.astype(f32).astype(bf16)

    def produce(p, carry):
        value = jnp.maximum(combine(products_h, p, 8) + b2, 0.0).astype(bf16)
        both = jnp.concatenate([value[:, :128], value[:, 128:]], axis=0)
        both = dot(both, spread).astype(bf16)
        refined[2 * p] = both[:channels]
        refined[2 * p + 1] = both[channels:]
        return carry

    lax.fori_loop(0, 2 * pairs, produce, 0, unroll=4)


def per_device(
    coarse_feats, fine_feats, pair_prior, zoom_start, coarse_weights, coarse_bias,
    refine_first, refine_second, refine_bias,
):
    channels, rows, cols = pair_prior.shape
    row_count = lax.axis_size("row")
    col_count = lax.axis_size("col")
    bins = rows * row_count
    row_place = lax.axis_index("row")
    col_place = lax.axis_index("col")
    pos = jnp.stack(
        [row_place, col_place, jnp.int32(rows), jnp.int32(cols), jnp.int32(bins)]
    ).astype(jnp.int32)
    odd_row = row_place % 2 == 1
    devices = row_count * col_count

    own = jnp.concatenate([coarse_feats, fine_feats], axis=0).T
    spread = jnp.broadcast_to(own[None], (devices,) + own.shape)
    feats = lax.all_to_all(spread, ("row", "col"), split_axis=0, concat_axis=0, tiled=True)
    feats = feats.reshape(bins, 2 * channels)

    def row_swap(block, rim):
        top, bottom = block[:rim], block[block.shape[0] - rim :]
        first, second = swap_pairs(row_count)
        return (
            lax.ppermute(jnp.where(odd_row, top, bottom), "row", first),
            lax.ppermute(jnp.where(odd_row, bottom, top), "row", second),
        )

    def col_swap(a, b):
        first, second = swap_pairs(col_count)
        return lax.ppermute(a, "col", first), lax.ppermute(b, "col", second)

    def struct(shape, dtype=bf16):
        return jax.ShapeDtypeStruct(shape, dtype)

    rim = 6
    center = jnp.transpose(pair_prior, (1, 0, 2))
    row_a, row_b = row_swap(center, rim)
    total = rows + 2 * rim
    pack = struct((pl.cdiv(total, 16), channels, 128))
    col_a, col_b = col_swap(
        *call(strip_pack_tile, (pack, pack), [], (1 << 20, 2 << 20), "tile_strips")(
            pos, center, row_a, row_b
        )
    )
    stacked = 3 * channels

    message = struct((rows // 4, channels, 128))
    coarse, *messages = call(
        tile_kernel,
        (struct((rows, channels, cols)),) + (message,) * 4,
        [
            pltpu.VMEM((total, stacked, 256), bf16),
            pltpu.VMEM((total, stacked, 256), bf16),
            pltpu.VMEM((total, stacked, 256), f32),
            pltpu.VMEM((channels, 128), f32),
        ],
        (3 << 30, 4 << 20),
        "tile",
    )(
        pos,
        coarse_weights.reshape(2, stacked, stacked),
        coarse_bias[:, :, None],
        feats, center, row_a, row_b, col_a, col_b,
    )

    half_rows, half_cols = row_count // 2, col_count // 2
    received = []
    for u in range(2):
        for v in range(2):
            pairs = []
            for a in range(half_rows):
                for b in range(half_cols):
                    pairs.append((a * col_count + b, (2 * a + u) * col_count + 2 * b + v))
                    pairs.append(
                        (
                            (half_rows + a) * col_count + half_cols + b,
                            (2 * a + 1 - u) * col_count + 2 * b + 1 - v,
                        )
                    )
            received.append(lax.ppermute(messages[2 * u + v], ("row", "col"), pairs))
    quarter = 2 * (row_place % 2) + col_place % 2
    quarter = jnp.where(zoom_start[0] > 0, 3 - quarter, quarter)
    window = jnp.where(
        quarter < 2,
        jnp.where(quarter == 0, received[0], received[1]),
        jnp.where(quarter == 2, received[2], received[3]),
    )

    parts = refine_first.reshape(3, channels, 3, 2 * channels)
    window_weights = parts[..., :channels].reshape(stacked, stacked)
    fine_parts = parts[..., channels:]
    row_terms, col_terms = call(
        fine_kernel,
        (struct((rows + 32, channels, 128), f32), struct((2, 3, channels, 128), f32)),
        [pltpu.VMEM((stacked, 128), f32)],
        (1 << 28, 4 << 20),
        "fine",
    )(
        pos,
        fine_parts.transpose(2, 1, 0, 3).reshape(stacked, stacked),
        fine_parts.reshape(stacked, stacked),
        refine_bias[0][:, None],
        feats,
    )

    window_rim = 6
    row_a, row_b = row_swap(window, window_rim)
    pairs = rows // 4 + 2 * window_rim
    pack = struct((pairs // 4, channels, 128))
    col_a, col_b = col_swap(
        *call(strip_pack_window, (pack, pack), [], (1 << 20, 1 << 20), "window_strips")(
            pos, window, row_a, row_b
        )
    )
    fine_rows = rows // 2 + 16
    refined = call(
        refine_kernel,
        struct((rows, channels, cols)),
        [
            pltpu.VMEM((pairs, stacked, 256), bf16),
            pltpu.VMEM((fine_rows, stacked, 256), bf16),
            pltpu.VMEM((pairs, stacked, 256), f32),
            pltpu.VMEM((fine_rows, stacked, 256), f32),
        ],
        (3 << 30, 6 << 20),
        "refine",
    )(
        pos,
        window_weights,
        refine_second.reshape(stacked, stacked),
        refine_bias[1][:, None],
        window, row_a, row_b, col_a, col_b, row_terms, col_terms,
    )
    return jnp.transpose(coarse, (1, 0, 2)), jnp.transpose(refined, (1, 0, 2))


def solution(mesh):
    return jax.shard_map(
        per_device,
        mesh=mesh,
        in_specs=(
            P(None, ("row", "col")),
            P(None, ("row", "col")),
            P(None, "row", "col"),
            P(),
            P(),
            P(),
            P(),
            P(),
            P(),
        ),
        out_specs=(P(None, "row", "col"), P(None, "row", "col")),
        check_vma=False,
    )
```

time: 443 us -> 147 us (0.33)
  the two profiles are of different devices: /device:TPU:10 before, /device:TPU:13 now
where the time goes in v1:
time: 147 us; the launch traced here: 146 us
  Pallas kernels  68.7 us (47%)
  starting transfers between devices  39.5 us (27%)
  waiting for transfers between devices  20 us (14%)
  local copies, waits for them, and re-layouts  16 us (11%)
    pallas_call x5, Pallas kernels, run(): pl.pallas_call(body, out_shape=outs, in_specs=[SMEM] + [VMEM] * (len(args...  68.7 us
    ppermute x4, waiting for transfers between devices, per_device(): received.append(lax.ppermute(messages[2 * u + v], ('row', 'col'), pairs))  16.1 us
    ppermute x4, starting transfers between devices, col_swap(): return (lax.ppermute(a, 'col', first), lax.ppermute(b, 'col', second))  13.6 us
    ppermute x2, starting transfers between devices, row_swap(): lax.ppermute(jnp.where(odd_row, top, bottom), 'row', first)  10.3 us
    unnamed x35, local copies, waits for them, and re-layouts  9.72 us
    all_to_all x1, starting transfers between devices, per_device(): lax.all_to_all(spread, ('row', 'col'), split_axis=0, concat_axis=0, tiled...  6.27 us
    ppermute x2, starting transfers between devices, row_swap(): lax.ppermute(jnp.where(odd_row, bottom, top), 'row', second)  5.29 us
    ppermute x4, starting transfers between devices, per_device(): received.append(lax.ppermute(messages[2 * u + v], ('row', 'col'), pairs))  4.07 us
  transfers between devices with their start and end apart: 13, of which 5 were waited for; matrix products, arithmetic and copies ran while one was open for 6% of the time, Pallas kernels for 12%

profile of v1, /device:TPU:13, one launch (start us, length us, event | category | flops | bytes accessed | tf_op | source)
XLA Modules:
  0.0 146.1 jit_solution(8117897222081013050)
XLA Ops:
  0.6 0.0 copy-start.9
  0.6 0.8 maximum_bitcast_fusion
  1.4 0.7 broadcast_in_dim.10
  2.1 6.3 %all-to-all-start = ((bf16[32,16,128]{2,1,0:T(8,128)(2,1)}), bf16[32,16,128]{2,1,0:T(8,128)(2,1)S(1)}, u32[]{:S(2)}, u32[]{:S(2)}) async-start(bf16[32,16,128]{2,1,0:T(8,128)(2,1)} %broadcast_in_dim.10), calls=%async_computation | async-start | bytes 262144 | tf_op jit(solution)/shard_map/all_to_all | solution.py:379
  8.4 1.9 %copy.26 = bf16[64,64,128]{2,0,1:T(8,128)(2,1)S(1)} copy(bf16[64,64,128]{2,1,0:T(8,128)(2,1)} %param.11) | data formatting | bytes 2097152 | tf_op args[2]
  10.3 0.0 copy-start
  10.3 3.4 %collective-permute-start.1 = (bf16[6,64,128]{2,1,0:T(8,128)(2,1)S(1)}, bf16[6,64,128]{2,1,0:T(8,128)(2,1)S(1)}, u32[]{:S(2)}, u32[]{:S(2)}) collective-permute-start(bf16[6,64,128]{2,1,0:T(8,128)(2,1)S(1)} %get-tuple-element.28), channel_id=1, source_target_pairs={{4,8},{12,16},{20,24},{8,4},{16,12},{24,20},{5,9},{13,17},{21,25},... | collective-permute-start | bytes 294920 | tf_op jit(solution)/shard_map/ppermute | solution.py:387
  13.7 0.2 collective-permute-start
  13.9 0.7 stack.11.pos
  14.6 2.0 %collective-permute-done.1.row_b = bf16[6,64,128]{2,1,0:T(8,128)(2,1)S(1)} collective-permute-done((bf16[6,64,128]{2,1,0:T(8,128)(2,1)S(1)}, bf16[6,64,128]{2,1,0:T(8,128)(2,1)S(1)}, u32[]{:S(2)}, u32[]{:S(2)}) %collective-permute-start.1) | collective-permute-done | bytes 98336 | tf_op jit(solution)/shard_map/ppermute | solution.py:387
  16.6 0.0 collective-permute-done.row_a
  16.6 0.0 copy-done
  16.6 0.6 copy-done.5
  17.2 0.6 copy-done.6
  17.8 7.2 %tile_strips.1 = (bf16[5,64,128]{2,1,0:T(8,128)(2,1)}, bf16[5,64,128]{2,1,0:T(8,128)(2,1)}) custom-call(s32[5]{0:T(128)} %stack.11.pos, bf16[64,64,128]{2,1,0:T(8,128)(2,1)} %bitcast.22, bf16[6,64,128]{2,1,0:T(8,128)(2,1)} %copy-done.6, bf16[6,64,128]{2,1,0:T(8,128)(2,1)} %copy-done.5), custom_call_target="tpu_custom_call" | custom-call | flops 1048576 | bytes 2097152 | tf_op jit(solution)/shard_map/tile_strips/pallas_call | solution.py:17
  25.0 0.4 collective-permute-start.2
  25.4 4.0 %collective-permute-start.3 = (bf16[5,64,128]{2,1,0:T(8,128)(2,1)}, bf16[5,64,128]{2,1,0:T(8,128)(2,1)S(1)}, u32[]{:S(2)}, u32[]{:S(2)}) collective-permute-start(bf16[5,64,128]{2,1,0:T(8,128)(2,1)} %get-tuple-element.14), channel_id=1, source_target_pairs={{1,2},{2,1},{5,6},{6,5},{9,10},{10,9},{13,14},{14,13},{17,18},{18,... | collective-permute-start | bytes 245768 | tf_op jit(solution)/shard_map/ppermute | solution.py:392
  29.4 0.0 copy-done.9
  29.4 0.7 copy.19.bias
  30.1 0.0 collective-permute-done.2.col_a
  30.1 1.3 collective-permute-done.3.col_b
  31.4 0.0 all-to-all-done
  31.4 0.0 copy-done.13
  31.4 0.6 copy-done.14
  32.0 0.1 copy-done.4
  32.1 29.7 %tile.1 = (bf16[64,64,128]{2,1,0:T(8,128)(2,1)}, bf16[16,64,128]{2,1,0:T(8,128)(2,1)}, bf16[16,64,128]{2,1,0:T(8,128)(2,1)}, bf16[16,64,128]{2,1,0:T(8,128)(2,1)}, bf16[16,64,128]{2,1,0:T(8,128)(2,1)}) custom-call(s32[5]{0:T(128)} %stack.11.pos, bf16[2,192,192]{2,1,0:T(8,128)(2,1)} %bitcast.29, f32[2,64,1]{2,1,0:T(8,128)} %copy.19.bias, ...), custom_call_target="tpu_custom_call" | custom-call | flops 3221225472 | bytes 4194304 | tf_op jit(solution)/shard_map/tile/pallas_call | solution.py:17
  61.9 1.4 collective-permute-start.4
  63.3 0.7 collective-permute-start.5
  64.0 0.7 collective-permute-start.6
  64.7 1.3 collective-permute-start.7
  66.0 0.0 copy-done.15
  66.0 0.0 copy-done.3
  66.1 8.8 %collective-permute-done.4 = bf16[16,64,128]{2,1,0:T(8,128)(2,1)S(1)} collective-permute-done((bf16[16,64,128]{2,1,0:T(8,128)(2,1)}, bf16[16,64,128]{2,1,0:T(8,128)(2,1)S(1)}, u32[]{:S(2)}, u32[]{:S(2)}) %collective-permute-start.4) | collective-permute-done | bytes 262176 | tf_op jit(solution)/shard_map/ppermute | solution.py:442
  74.8 0.0 collective-permute-done.5
  74.8 0.0 collective-permute-done.6
  74.8 7.3 %collective-permute-done.7 = bf16[16,64,128]{2,1,0:T(8,128)(2,1)S(1)} collective-permute-done((bf16[16,64,128]{2,1,0:T(8,128)(2,1)}, bf16[16,64,128]{2,1,0:T(8,128)(2,1)S(1)}, u32[]{:S(2)}, u32[]{:S(2)}) %collective-permute-start.7) | collective-permute-done | bytes 262176 | tf_op jit(solution)/shard_map/ppermute | solution.py:442
  82.2 0.0 copy-start.1
  82.2 1.9 %collective-permute-start.9 = (bf16[6,64,128]{2,1,0:T(8,128)(2,1)S(1)}, bf16[6,64,128]{2,1,0:T(8,128)(2,1)S(1)}, u32[]{:S(2)}, u32[]{:S(2)}) collective-permute-start(bf16[6,64,128]{2,1,0:T(8,128)(2,1)S(1)} %get-tuple-element.30), channel_id=1, source_target_pairs={{4,8},{12,16},{20,24},{8,4},{16,12},{24,20},{5,9},{13,17},{21,25},... | collective-permute-start | bytes 294920 | tf_op jit(solution)/shard_map/ppermute | solution.py:387
  84.2 10.1 %collective-permute-start.8 = (bf16[6,64,128]{2,1,0:T(8,128)(2,1)S(1)}, bf16[6,64,128]{2,1,0:T(8,128)(2,1)S(1)}, u32[]{:S(2)}, u32[]{:S(2)}) collective-permute-start(bf16[6,64,128]{2,1,0:T(8,128)(2,1)S(1)} %get-tuple-element.31), channel_id=1, source_target_pairs={{0,4},{4,0},{8,12},{12,8},{16,20},{20,16},{24,28},{28,24},{1,5},{5... | collective-permute-start | bytes 294920 | tf_op jit(solution)/shard_map/ppermute | solution.py:386
  94.3 0.2 fusion
  94.5 0.0 collective-permute-done.9.row_b
  94.5 0.0 copy-start.7
  94.5 0.7 collective-permute-done.8.row_a
  95.2 0.0 copy-done.1
  95.2 0.0 copy-done.7
  95.2 0.6 copy-done.8
  95.9 3.0 %window_strips.1 = (bf16[7,64,128]{2,1,0:T(8,128)(2,1)}, bf16[7,64,128]{2,1,0:T(8,128)(2,1)}) custom-call(s32[5]{0:T(128)} %stack.11.pos, bf16[16,64,128]{2,1,0:T(8,128)(2,1)} %copy-done.1, bf16[6,64,128]{2,1,0:T(8,128)(2,1)} %copy-done.8, bf16[6,64,128]{2,1,0:T(8,128)(2,1)} %copy-done.7), custom_call_target="tpu_custom_call" | custom-call | flops 1048576 | bytes 1048576 | tf_op jit(solution)/shard_map/window_strips/pallas_call | solution.py:17
  98.9 0.0 collective-permute-start.10
  98.9 9.2 %collective-permute-start.11 = (bf16[7,64,128]{2,1,0:T(8,128)(2,1)}, bf16[7,64,128]{2,1,0:T(8,128)(2,1)S(1)}, u32[]{:S(2)}, u32[]{:S(2)}) collective-permute-start(bf16[7,64,128]{2,1,0:T(8,128)(2,1)} %get-tuple-element.21), channel_id=1, source_target_pairs={{1,2},{2,1},{5,6},{6,5},{9,10},{10,9},{13,14},{14,13},{17,18},{18,... | collective-permute-start | bytes 344072 | tf_op jit(solution)/shard_map/ppermute | solution.py:392
  108.1 0.0 copy-done.10
  108.1 0.7 copy.21.bias
  108.8 0.7 copy.22.bias2
  109.5 0.8 reshape.34.col_weights
  110.3 0.8 reshape.31.weights
  111.1 0.2 copy.20
  111.3 0.8 reshape.33.row_weights
  112.1 1.6 %copy.23 = bf16[64,64,128]{2,1,0:T(8,128)(2,1)} copy(bf16[64,64,128]{2,0,1:T(8,128)(2,1)S(1)} %bitcast.24) | data formatting | bytes 2097152
  113.7 10.8 %fine.1 = (f32[96,64,128]{2,1,0:T(8,128)}, f32[2,3,64,128]{3,2,1,0:T(8,128)}) custom-call(s32[5]{0:T(128)} %stack.11.pos, bf16[192,192]{1,0:T(8,128)(2,1)} %reshape.33.row_weights, bf16[192,192]{1,0:T(8,128)(2,1)} %reshape.34.col_weights, f32[64,1]{1,0:T(8,128)} %copy.21.bias, bf16[512,128]{1,0:T(8,128)(2,1)} %bitcast.27), custom_call_target="tpu_custom_call" | custom-call | flops 268435456 | bytes 4194304 | tf_op jit(solution)/shard_map/fine/pallas_call | solution.py:17
  124.5 0.0 collective-permute-done.10.col_a
  124.5 0.0 collective-permute-done.11.col_b
  124.6 0.6 copy-done.11
  125.2 0.1 copy-done.12
  125.2 17.9 %refine.1 = bf16[64,64,128]{2,1,0:T(8,128)(2,1)} custom-call(s32[5]{0:T(128)} %stack.11.pos, bf16[192,192]{1,0:T(8,128)(2,1)} %reshape.31.weights, bf16[192,192]{1,0:T(8,128)(2,1)} %bitcast.30, f32[64,1]{1,0:T(8,128)} %copy.22.bias2, bf16[16,64,128]{2,1,0:T(8,128)(2,1)} %copy-done.1, bf16[6,64,128]{2,1,0:T(8,128)(2,1)} %copy-done.8, ...), custom_call_target="tpu_custom_call" | custom-call | flops 3221225472 | bytes 6291456 | tf_op jit(solution)/shard_map/refine/pallas_call | solution.py:17
  143.2 2.9 %copy.24 = bf16[64,64,128]{2,1,0:T(8,128)(2,1)} copy(bf16[64,64,128]{2,0,1:T(8,128)(2,1)} %bitcast.25) | data formatting | bytes 2097152
  (18 shorter events, 0.2 us)
Async XLA Ops:
  0.6 28.8 %copy-start.9 = (f32[2,64]{1,0:T(2,128)S(1)}, f32[2,64]{1,0:T(2,128)}, u32[]{:S(2)}) copy-start(f32[2,64]{1,0:T(2,128)} %param.14) | copy-start | bytes 1540
  2.1 29.3 %all-to-all-start = ((bf16[32,16,128]{2,1,0:T(8,128)(2,1)}), bf16[32,16,128]{2,1,0:T(8,128)(2,1)S(1)}, u32[]{:S(2)}, u32[]{:S(2)}) async-start(bf16[32,16,128]{2,1,0:T(8,128)(2,1)} %broadcast_in_dim.10), calls=%async_computation | async-start | bytes 262144 | tf_op jit(solution)/shard_map/all_to_all | solution.py:379
  10.3 6.3 %copy-start = (bf16[64,64,128]{2,0,1:T(8,128)(2,1)}, bf16[64,64,128]{2,0,1:T(8,128)(2,1)S(1)}, u32[]{:S(2)}) copy-start(bf16[64,64,128]{2,0,1:T(8,128)(2,1)S(1)} %copy.26) | copy-start | bytes 3145732
  10.3 6.2 %collective-permute-start.1 = (bf16[6,64,128]{2,1,0:T(8,128)(2,1)S(1)}, bf16[6,64,128]{2,1,0:T(8,128)(2,1)S(1)}, u32[]{:S(2)}, u32[]{:S(2)}) collective-permute-start(bf16[6,64,128]{2,1,0:T(8,128)(2,1)S(1)} %get-tuple-element.28), channel_id=1, source_target_pairs={{4,8},{12,16},{20,24},{8,4},{16,12},{24,20},{5,9},{13,17},{21,25},... | collective-permute-start | bytes 294920 | tf_op jit(solution)/shard_map/ppermute | solution.py:387
  13.7 2.9 %collective-permute-start = (bf16[6,64,128]{2,1,0:T(8,128)(2,1)S(1)}, bf16[6,64,128]{2,1,0:T(8,128)(2,1)S(1)}, u32[]{:S(2)}, u32[]{:S(2)}) collective-permute-start(bf16[6,64,128]{2,1,0:T(8,128)(2,1)S(1)} %get-tuple-element.29), channel_id=1, source_target_pairs={{0,4},{4,0},{8,12},{12,8},{16,20},{20,16},{24,28},{28,24},{1,5},{5... | collective-permute-start | bytes 294920 | tf_op jit(solution)/shard_map/ppermute | solution.py:386
  16.6 0.6 copy-start.5
  17.2 0.6 copy-start.6
  25.0 5.1 %collective-permute-start.2 = (bf16[5,64,128]{2,1,0:T(8,128)(2,1)}, bf16[5,64,128]{2,1,0:T(8,128)(2,1)S(1)}, u32[]{:S(2)}, u32[]{:S(2)}) collective-permute-start(bf16[5,64,128]{2,1,0:T(8,128)(2,1)} %get-tuple-element.13), channel_id=1, source_target_pairs={{0,1},{1,0},{2,3},{3,2},{4,5},{5,4},{6,7},{7,6},{8,9},{9,8},{10,11... | collective-permute-start | bytes 245768 | tf_op jit(solution)/shard_map/ppermute | solution.py:392
  25.4 6.0 %collective-permute-start.3 = (bf16[5,64,128]{2,1,0:T(8,128)(2,1)}, bf16[5,64,128]{2,1,0:T(8,128)(2,1)S(1)}, u32[]{:S(2)}, u32[]{:S(2)}) collective-permute-start(bf16[5,64,128]{2,1,0:T(8,128)(2,1)} %get-tuple-element.14), channel_id=1, source_target_pairs={{1,2},{2,1},{5,6},{6,5},{9,10},{10,9},{13,14},{14,13},{17,18},{18,... | collective-permute-start | bytes 245768 | tf_op jit(solution)/shard_map/ppermute | solution.py:392
  30.1 1.3 copy-start.13
  31.4 0.6 copy-start.14
  31.4 0.7 copy-start.4
  32.1 33.9 %copy-start.15 = (s32[2]{0:T(128)S(1)}, s32[2]{0:T(128)}, u32[]{:S(2)}) copy-start(s32[2]{0:T(128)} %param.12) | copy-start | bytes 28
  32.1 33.9 %copy-start.3 = (bf16[3,64,384]{2,1,0:T(8,128)(2,1)S(1)}, bf16[3,64,384]{2,1,0:T(8,128)(2,1)}, u32[]{:S(2)}) copy-start(bf16[3,64,384]{2,1,0:T(8,128)(2,1)} %param.15) | copy-start | bytes 442372
  61.8 46.2 %copy-start.10 = (f32[2,64]{1,0:T(2,128)S(1)}, f32[2,64]{1,0:T(2,128)}, u32[]{:S(2)}) copy-start(f32[2,64]{1,0:T(2,128)} %param.17) | copy-start | bytes 1540
  61.8 50.2 %copy-start.2 = (bf16[64,64,128]{2,1,0:T(8,128)(2,1)S(1)}, bf16[64,64,128]{2,1,0:T(8,128)(2,1)}, u32[]{:S(2)}) copy-start(bf16[64,64,128]{2,1,0:T(8,128)(2,1)} %get-tuple-element.15) | copy-start | bytes 3145732
  61.9 13.0 %collective-permute-start.4 = (bf16[16,64,128]{2,1,0:T(8,128)(2,1)}, bf16[16,64,128]{2,1,0:T(8,128)(2,1)S(1)}, u32[]{:S(2)}, u32[]{:S(2)}) collective-permute-start(bf16[16,64,128]{2,1,0:T(8,128)(2,1)} %get-tuple-element.16), channel_id=1, source_target_pairs={{0,0},{18,5},{1,2},{19,7},{4,8},{22,13},{5,10},{23,15},{8,16},{26,... | collective-permute-start | bytes 786440 | tf_op jit(solution)/shard_map/ppermute | solution.py:442
  63.3 11.6 %collective-permute-start.5 = (bf16[16,64,128]{2,1,0:T(8,128)(2,1)}, bf16[16,64,128]{2,1,0:T(8,128)(2,1)S(1)}, u32[]{:S(2)}, u32[]{:S(2)}) collective-permute-start(bf16[16,64,128]{2,1,0:T(8,128)(2,1)} %get-tuple-element.17), channel_id=1, source_target_pairs={{0,1},{18,4},{1,3},{19,6},{4,9},{22,12},{5,11},{23,14},{8,17},{26,... | collective-permute-start | bytes 786440 | tf_op jit(solution)/shard_map/ppermute | solution.py:442
  64.0 10.9 %collective-permute-start.6 = (bf16[16,64,128]{2,1,0:T(8,128)(2,1)}, bf16[16,64,128]{2,1,0:T(8,128)(2,1)S(1)}, u32[]{:S(2)}, u32[]{:S(2)}) collective-permute-start(bf16[16,64,128]{2,1,0:T(8,128)(2,1)} %get-tuple-element.18), channel_id=1, source_target_pairs={{0,4},{18,1},{1,6},{19,3},{4,12},{22,9},{5,14},{23,11},{8,20},{26,... | collective-permute-start | bytes 786440 | tf_op jit(solution)/shard_map/ppermute | solution.py:442
  64.7 17.5 %collective-permute-start.7 = (bf16[16,64,128]{2,1,0:T(8,128)(2,1)}, bf16[16,64,128]{2,1,0:T(8,128)(2,1)S(1)}, u32[]{:S(2)}, u32[]{:S(2)}) collective-permute-start(bf16[16,64,128]{2,1,0:T(8,128)(2,1)} %get-tuple-element.19), channel_id=1, source_target_pairs={{0,5},{18,0},{1,7},{19,2},{4,13},{22,8},{5,15},{23,10},{8,21},{26,... | collective-permute-start | bytes 786440 | tf_op jit(solution)/shard_map/ppermute | solution.py:442
  82.2 13.0 %copy-start.1 = (bf16[16,64,128]{2,1,0:T(8,128)(2,1)}, bf16[16,64,128]{2,1,0:T(8,128)(2,1)S(1)}, u32[]{:S(2)}) copy-start(bf16[16,64,128]{2,1,0:T(8,128)(2,1)S(1)} %select_select_fusion.center) | copy-start | bytes 786436
  82.2 12.3 %collective-permute-start.9 = (bf16[6,64,128]{2,1,0:T(8,128)(2,1)S(1)}, bf16[6,64,128]{2,1,0:T(8,128)(2,1)S(1)}, u32[]{:S(2)}, u32[]{:S(2)}) collective-permute-start(bf16[6,64,128]{2,1,0:T(8,128)(2,1)S(1)} %get-tuple-element.30), channel_id=1, source_target_pairs={{4,8},{12,16},{20,24},{8,4},{16,12},{24,20},{5,9},{13,17},{21,25},... | collective-permute-start | bytes 294920 | tf_op jit(solution)/shard_map/ppermute | solution.py:387
  84.2 11.0 %collective-permute-start.8 = (bf16[6,64,128]{2,1,0:T(8,128)(2,1)S(1)}, bf16[6,64,128]{2,1,0:T(8,128)(2,1)S(1)}, u32[]{:S(2)}, u32[]{:S(2)}) collective-permute-start(bf16[6,64,128]{2,1,0:T(8,128)(2,1)S(1)} %get-tuple-element.31), channel_id=1, source_target_pairs={{0,4},{4,0},{8,12},{12,8},{16,20},{20,16},{24,28},{28,24},{1,5},{5... | collective-permute-start | bytes 294920 | tf_op jit(solution)/shard_map/ppermute | solution.py:386
  94.5 0.7 copy-start.7
  95.2 0.6 copy-start.8
  98.9 25.7 %collective-permute-start.10 = (bf16[7,64,128]{2,1,0:T(8,128)(2,1)}, bf16[7,64,128]{2,1,0:T(8,128)(2,1)S(1)}, u32[]{:S(2)}, u32[]{:S(2)}) collective-permute-start(bf16[7,64,128]{2,1,0:T(8,128)(2,1)} %get-tuple-element.20), channel_id=1, source_target_pairs={{0,1},{1,0},{2,3},{3,2},{4,5},{5,4},{6,7},{7,6},{8,9},{9,8},{10,11... | collective-permute-start | bytes 344072 | tf_op jit(solution)/shard_map/ppermute | solution.py:392
  98.9 25.7 %collective-permute-start.11 = (bf16[7,64,128]{2,1,0:T(8,128)(2,1)}, bf16[7,64,128]{2,1,0:T(8,128)(2,1)S(1)}, u32[]{:S(2)}, u32[]{:S(2)}) collective-permute-start(bf16[7,64,128]{2,1,0:T(8,128)(2,1)} %get-tuple-element.21), channel_id=1, source_target_pairs={{1,2},{2,1},{5,6},{6,5},{9,10},{10,9},{13,14},{14,13},{17,18},{18,... | collective-permute-start | bytes 344072 | tf_op jit(solution)/shard_map/ppermute | solution.py:392
  124.5 0.6 copy-start.11
  124.6 0.7 copy-start.12

commit v2 on v1

v2 whole, which is shorter than its diff:
```python
import functools

import jax
import jax.numpy as jnp
from jax import lax
from jax.experimental import pallas as pl
from jax.experimental.pallas import tpu as pltpu
from jax.sharding import PartitionSpec as P

f32 = jnp.float32
bf16 = jnp.bfloat16
VMEM = pl.BlockSpec(memory_space=pltpu.VMEM)
SMEM = pl.BlockSpec(memory_space=pltpu.SMEM)


def call(body, outs, scratch, cost, name):
    flops, moved = cost
    def run(*args):
        return pl.pallas_call(
            body,
            out_shape=outs,
            in_specs=[SMEM] + [VMEM] * (len(args) - 1),
            out_specs=jax.tree.map(lambda _: VMEM, outs),
            scratch_shapes=scratch,
            compiler_params=pltpu.CompilerParams(vmem_limit_bytes=56 << 20),
            cost_estimate=pl.CostEstimate(flops=flops, bytes_accessed=moved, transcendentals=0),
            name=name,
        )(*args)

    return run


def roll(x, shift):
    shift = shift % x.shape[-1]
    return x if shift == 0 else pltpu.roll(x, shift, x.ndim - 1)


def lanes(shape):
    return lax.broadcasted_iota(jnp.int32, shape, len(shape) - 1)


def swap_pairs(count):
    first = [(i, i ^ 1) for i in range(count)]
    second = [(i, i + 1) for i in range(1, count - 1, 2)]
    return first, second + [(b, a) for a, b in second]


def dot(a, b):
    return jnp.dot(a, b, preferred_element_type=f32)


def one_hot(hit):
    return hit.astype(f32).astype(bf16)


def pick_at(feats, index):
    shape = (feats.shape[1], 128)
    return dot(feats, one_hot(lax.broadcasted_iota(jnp.int32, shape, 0) == index))


def pick_bins(feats, start, step):
    return pick_at(feats, start + step * lanes((1, 128)))


def source_and_target(sources, targets):
    shape = (sources, targets)
    return lax.broadcasted_iota(jnp.int32, shape, 0), lanes(shape)


def within(at, bins):
    return ((at >= 0) & (at < bins)).astype(f32)


def inside(start, step, bins, shape=(1, 128)):
    at = start + step * lanes(shape)
    return ((at >= 0) & (at < bins)).astype(f32)


def scalar_inside(at, bins):
    return ((at >= 0) & (at < bins)).astype(f32)


def ext_row(e, odd_row, center, row_a, row_b):
    rim, count = row_a.shape[0], center.shape[0]
    if e < rim:
        return jnp.where(odd_row, row_a[e], row_b[e])
    if e < rim + count:
        return center[e - rim]
    return jnp.where(odd_row, row_b[e - rim - count], row_a[e - rim - count])


def pair_kernel(pos, feats, center, row_a, row_b, pair, out_a, out_b, own_feats):
    rim, channels, width = row_a.shape
    rows = center.shape[0]
    bins = feats.shape[1]
    row_start = pos[0] * rows
    odd_row = pos[0] % 2 == 1
    odd_col = pos[1] % 2 == 1
    total = rows + 2 * rim
    all_feats = feats[:channels]
    own_feats[...] = pick_bins(all_feats, row_start - rim, 1)
    col_feats = pick_bins(all_feats, pos[1] * width, 1)
    source, target = source_and_target(width, 2 * width)
    last = (target >= width) == odd_col
    copies = one_hot(source == target % 8 + jnp.where(last, width - 8, 0))
    slot = lanes((channels, width)) // 8
    for group in range(out_a.shape[0]):
        size = min(16, total - group * 16)
        blocks = []
        for k in range(size):
            e = group * 16 + k
            x = ext_row(e, odd_row, center, row_a, row_b).astype(f32)
            value = x + (col_feats + own_feats[:, e : e + 1])
            if e < rim or e >= rim + rows:
                value = value * scalar_inside(row_start - rim + e, bins)
            blocks.append(value.astype(bf16))
            pair[e] = blocks[-1]
        spread = dot(jnp.concatenate(blocks, axis=0), copies)
        for out, first in ((out_a, 0), (out_b, width)):
            parts = [
                jnp.where(
                    slot == k,
                    spread[k * channels : (k + 1) * channels, first : first + width],
                    0.0,
                )
                for k in range(size)
            ]
            while len(parts) > 1:
                parts = [sum(parts[i : i + 2]) for i in range(0, len(parts), 2)]
            out[group] = parts[0].astype(bf16)


def products(weights, taps, out, count):
    def one(row, carry):
        out[row] = dot(weights, taps[row])
        return carry

    lax.fori_loop(0, count, one, 0, unroll=4)


def combine(parts, row, spacing):
    size = parts.shape[1] // 3
    return (
        parts[row, :size]
        + parts[row + spacing, size : 2 * size]
        + parts[row + 2 * spacing, 2 * size :]
    )


def tile_kernel(
    turn, pos, weights, bias, pair, col_a, col_b, m0, m1, s1, s2, parts,
):
    total, channels, width = pair.shape
    half = width // 2
    rows, bins = pos[2], pos[4]
    rim = 6
    row_start = pos[0] * rows
    col_start = pos[1] * width
    odd_col = pos[1] % 2 == 1
    upper = 2 * row_start < bins
    first_col = half * jnp.where(upper, turn, 1 - turn) - rim
    lane = lanes((channels, width))
    slot = lane // 8
    source, target = source_and_target(2 * width, 3 * width)
    col = target % width + 2 * (target // width) + first_col
    inner = (source == col) & (source < width)
    strip = source - width
    near = strip < half
    on_left = (strip % 8 == col + 8) & (col < 0)
    on_right = (strip % 8 == col - width) & (col >= width)
    strip_ok = strip >= 0
    move = [
        one_hot(inner | (strip_ok & ((near & on_left) | (~near & on_right)))),
        one_hot(inner | (strip_ok & ((~near & on_left) | (near & on_right)))),
    ]
    for group in range(col_a.shape[0]):
        pa = col_a[group].astype(f32)
        pb = col_b[group].astype(f32)
        left = jnp.where(odd_col, pa, pb)
        right = roll(jnp.where(odd_col, pb, pa), half)
        for quad in range(4):
            blocks = []
            for k in range(4 * quad, 4 * quad + 4):
                e = 16 * group + k
                if e >= total:
                    break
                edge = jnp.where(slot == k, left, jnp.where(slot == (k + 8) % 16, right, 0.0))
                blocks.append(jnp.concatenate([pair[e], edge.astype(bf16)], axis=1))
            if not blocks:
                break
            moved = dot(jnp.concatenate(blocks, axis=0), move[quad // 2]).astype(bf16)
            for i in range(len(blocks)):
                e = 16 * group + 4 * quad + i
                for tap in range(3):
                    s1[
                        e // 2,
                        tap * channels : (tap + 1) * channels,
                        e % 2 * width : (e % 2 + 1) * width,
                    ] = moved[i * channels : (i + 1) * channels, tap * width : (tap + 1) * width]
    b1 = bias[0]
    mask1 = inside(col_start + first_col + 2, 1, bins)
    products(weights[0], s1, parts, total // 2)
    source, target = source_and_target(width, 2 * width)
    shift = one_hot(source == target % width + 4 * (target // width + 1))

    def first(c, carry):
        blocks = []
        for i in range(2):
            g = 2 * c + i
            value = jnp.maximum(combine(parts, g, 1) + b1, 0.0)
            for t in range(2):
                ok = scalar_inside(row_start - rim + 2 + 2 * g + t, bins)
                block = (value[:, t * width : (t + 1) * width] * (mask1 * ok)).astype(bf16)
                s2[g, :channels, t * width : (t + 1) * width] = block
                blocks.append(block)
        moved = dot(jnp.concatenate(blocks, axis=0), shift).astype(bf16)
        for j in range(4):
            for tap in (1, 2):
                s2[
                    2 * c + j // 2,
                    tap * channels : (tap + 1) * channels,
                    j % 2 * width : (j % 2 + 1) * width,
                ] = moved[j * channels : (j + 1) * channels, (tap - 1) * width : tap * width]
        return carry

    lax.fori_loop(0, (total - 4) // 4, first, 0, unroll=6)
    b2 = bias[1]
    products(weights[1], s2, parts, total // 2 - 2)
    low = lane < half
    quarter = m0.shape[0]
    for message, begin in (
        (m0, jnp.where(upper, 0, quarter)),
        (m1, jnp.where(upper, quarter, 0)),
    ):

        def produce(p, carry, message=message, begin=begin):
            value = jnp.maximum(combine(parts, begin + p, 2) + b2, 0.0)
            message[p] = jnp.where(low, value[:, :width], roll(value[:, width:], half)).astype(bf16)
            return carry

        lax.fori_loop(0, quarter, produce, 0, unroll=8)


def assemble_kernel(pos, m00, m01, m10, m11, coarse):
    quarter, channels, width = m00.shape
    half = width // 2
    upper = 2 * pos[0] < pos[4] // pos[2]
    low = lanes((channels, width)) < half
    for u in range(2):

        def pair(p, carry, u=u):
            sides = [
                jnp.where(upper, (m00, m01, m10, m11)[2 * u + v][p], (m11, m10, m01, m00)[2 * u + v][p])
                for v in range(2)
            ]
            left, right = [side.astype(f32) for side in sides]
            at = 2 * (quarter * u + p)
            coarse[at] = jnp.where(low, left, roll(right, half)).astype(bf16)
            coarse[at + 1] = jnp.where(low, roll(left, half), right).astype(bf16)
            return carry

        lax.fori_loop(0, quarter, pair, 0, unroll=4)


def strip_pack_window(pos, center, row_a, row_b, out_a, out_b):
    rim, channels, width = row_a.shape
    half = width // 2
    odd_row = pos[0] % 2 == 1
    odd_col = pos[1] % 2 == 1
    source, target = source_and_target(width, 2 * width)
    last = (target >= width) == odd_col
    spot = target % width
    copies = one_hot(
        source == spot // half * half + spot % 16 + jnp.where(last, half - 16, 0)
    )
    slot = lanes((channels, width)) % half // 16
    for group in range(out_a.shape[0]):
        block = jnp.concatenate(
            [ext_row(group * 4 + m, odd_row, center, row_a, row_b) for m in range(4)], axis=0
        )
        spread = dot(block, copies)
        for out, first in ((out_a, 0), (out_b, width)):
            parts = [spread[m * channels : (m + 1) * channels, first : first + width] for m in range(4)]
            out[group] = jnp.where(
                slot < 2,
                jnp.where(slot == 0, parts[0], parts[1]),
                jnp.where(slot == 2, parts[2], parts[3]),
            ).astype(bf16)


def fine_kernel(pos, row_weights, col_weights, bias, feats, row_terms, col_terms, terms):
    channels = bias.shape[0]
    bins = feats.shape[1]
    row_start = pos[0] * pos[2]
    col_start = pos[1] * pos[3]
    all_feats = feats[channels:]

    def stacked(start, step, shift):
        picked = pick_bins(all_feats, start, step)
        return jnp.concatenate([roll(picked, -shift * tap) for tap in range(3)], 0).astype(bf16)

    parts = dot(row_weights[...], stacked(row_start - 24, 1, 8))
    taps = [parts[e * channels : (e + 1) * channels] for e in range(3)]
    at_left = pos[1] == 0
    at = col_start - 16 + 2 * lanes((channels, 128))
    inside_taps = ((at_left) | (at < bins - 8)) & (jnp.logical_not(at_left) | (at >= 8))
    terms[0] = taps[0] + taps[1] + taps[2] + bias[...]
    terms[1] = taps[1] + jnp.where(at_left, taps[2], taps[0]) + bias[...]
    for n in range(row_terms.shape[0]):
        row_terms[n] = jnp.where(inside_taps, terms[0, :, n : n + 1], terms[1, :, n : n + 1])
    for v in range(2):
        across = dot(col_weights[...], stacked(col_start - 24 + v, 2, 4))
        for a in range(3):
            col_terms[v, a] = across[a * channels : (a + 1) * channels]


def refine_kernel(
    pos, weights, weights2, bias2, center, row_a, row_b, col_a, col_b, row_terms, col_terms,
    refined, sw, sh, products_w, products_h,
):
    pairs, channels, _ = center.shape
    rim = row_a.shape[0]
    rows, cols, bins = pos[2], pos[3], pos[4]
    row_start = pos[0] * rows
    col_start = pos[1] * cols
    odd_row = pos[0] % 2 == 1
    odd_col = pos[1] % 2 == 1
    total = pairs + 2 * rim
    slot = lanes((channels, 128)) % 64 // 16
    source, target = source_and_target(384, 768)
    tap, t = target // 128 % 3, target // 384
    col = target % 128 + 4 * tap - 12
    spot = source % 128
    same = spot // 64 == t
    place = source // 128
    move = one_hot(
        same
        & (
            ((place == 0) & (spot % 64 == col))
            | ((place == 1) & (spot % 16 == col + 16) & (col < 0))
            | ((place == 2) & (spot % 16 == col - 64) & (col >= 64))
        )
    )
    for group in range(col_a.shape[0]):
        pa, pb = col_a[group].astype(f32), col_b[group].astype(f32)
        left = jnp.where(odd_col, pa, pb)
        right = jnp.where(odd_col, pb, pa)
        blocks = []
        for m in range(4):
            x = ext_row(4 * group + m, odd_row, center, row_a, row_b)
            here = slot == m
            blocks.append(
                jnp.concatenate(
                    [x]
                    + [jnp.where(here, side, 0.0).astype(bf16) for side in (left, right)],
                    axis=1,
                )
            )
        moved = dot(jnp.concatenate(blocks, axis=0), move).astype(bf16)
        for m in range(4):
            for j in range(6):
                sw[
                    4 * group + m,
                    j % 3 * channels : (j % 3 + 1) * channels,
                    j // 3 * 128 : (j // 3 + 1) * 128,
                ] = moved[m * channels : (m + 1) * channels, j * 128 : (j + 1) * 128]
    w1 = weights[...]
    col_in = inside(col_start - 16, 2, bins)
    source, target = source_and_target(256, 384)
    spot = target % 128
    spread = one_hot(source == spot // 64 * 128 + spot % 64 + 8 * (target // 128))
    products(w1, sw, products_w, total)

    def first(n, carry):
        both = combine(products_w, n, 2)
        blocks = []
        for t in range(2):
            k = 2 * n + t
            base = both[:, t * 128 : t * 128 + 128]
            at = row_start - 16 + 2 * k
            above = scalar_inside(at - 8, bins)
            below = scalar_inside(at + 8, bins)
            mask = col_in * scalar_inside(at, bins)
            sums = [
                base + (col_terms[v, 1] + col_terms[v, 0] * above + col_terms[v, 2] * below)
                for v in range(2)
            ]
            for u in range(2):
                own = row_terms[2 * k + u]
                h = [(jnp.maximum(s + own, 0.0) * mask).astype(bf16) for s in sums]
                blocks.append(jnp.concatenate(h, axis=1))
        moved = dot(jnp.concatenate(blocks, axis=0), spread).astype(bf16)
        for j in range(4):
            for tap in range(3):
                sh[
                    2 * n + j // 2,
                    tap * channels : (tap + 1) * channels,
                    j % 2 * 128 : (j % 2 + 1) * 128,
                ] = moved[j * channels : (j + 1) * channels, tap * 128 : (tap + 1) * 128]
        return carry

    inner = total - 4
    lax.fori_loop(0, inner, first, 0, unroll=6)
    w2 = weights2[...]
    b2 = bias2[...]

    products(w2, sh, products_h, sh.shape[0])
    source, target = source_and_target(128, 128)
    weave = one_hot(2 * (source % 64) + source // 64 == target)

    def produce(p, carry):
        value = jnp.maximum(combine(products_h, p, 8) + b2, 0.0).astype(bf16)
        both = jnp.concatenate([value[:, :128], value[:, 128:]], axis=0)
        both = dot(both, weave).astype(bf16)
        refined[2 * p] = both[:channels]
        refined[2 * p + 1] = both[channels:]
        return carry

    lax.fori_loop(0, 2 * pairs, produce, 0, unroll=8)


def per_device(
    coarse_feats, fine_feats, pair_prior, zoom_start, coarse_weights, coarse_bias,
    refine_first, refine_second, refine_bias,
):
    channels, rows, cols = pair_prior.shape
    row_count = lax.axis_size("row")
    col_count = lax.axis_size("col")
    bins = rows * row_count
    row_place = lax.axis_index("row")
    col_place = lax.axis_index("col")
    pos = jnp.stack(
        [row_place, col_place, jnp.int32(rows), jnp.int32(cols), jnp.int32(bins)]
    ).astype(jnp.int32)
    odd_row = row_place % 2 == 1
    devices = row_count * col_count

    own = jnp.concatenate([coarse_feats, fine_feats], axis=0).T
    spread = jnp.broadcast_to(own[None], (devices,) + own.shape)
    feats = lax.all_to_all(spread, ("row", "col"), split_axis=0, concat_axis=0, tiled=True)
    feats = feats.reshape(bins, 2 * channels).T

    def row_swap(block, rim):
        top, bottom = block[:rim], block[block.shape[0] - rim :]
        first, second = swap_pairs(row_count)
        return (
            lax.ppermute(jnp.where(odd_row, top, bottom), "row", first),
            lax.ppermute(jnp.where(odd_row, bottom, top), "row", second),
        )

    def col_swap(a, b):
        first, second = swap_pairs(col_count)
        return lax.ppermute(a, "col", first), lax.ppermute(b, "col", second)

    def struct(shape, dtype=bf16):
        return jax.ShapeDtypeStruct(shape, dtype)

    rim = 6
    center = jnp.transpose(pair_prior, (1, 0, 2))
    row_a, row_b = row_swap(center, rim)
    total = rows + 2 * rim
    pack = struct((pl.cdiv(total, 16), channels, 128))
    pair, *packs = call(
        pair_kernel,
        (struct((total, channels, cols)), pack, pack),
        [pltpu.VMEM((channels, 128), f32)],
        (1 << 28, 4 << 20),
        "pair",
    )(pos, feats, center, row_a, row_b)
    col_a, col_b = col_swap(*packs)
    stacked = 3 * channels

    message = struct((rows // 4, channels, 128))
    tile_weights = coarse_weights.reshape(2, stacked, stacked)
    tile_bias = coarse_bias[:, :, None]
    halves = [
        call(
            functools.partial(tile_kernel, turn),
            (message,) * 2,
            [
                pltpu.VMEM((total // 2, stacked, 256), bf16),
                pltpu.VMEM((total // 2, stacked, 256), bf16),
                pltpu.VMEM((total // 2, stacked, 256), f32),
            ],
            (3 << 30, 3 << 20),
            f"tile{turn}",
        )(
            pos, tile_weights, tile_bias, pair, col_a, col_b
        )
        for turn in range(2)
    ]
    messages = [halves[v][u] for u in range(2) for v in range(2)]
    coarse = call(
        assemble_kernel, struct((rows, channels, cols)), [], (1 << 20, 2 << 20), "assemble"
    )(pos, *messages)

    half_rows, half_cols = row_count // 2, col_count // 2
    received = [None] * 4
    for v in range(2):
        for u in range(2):
            pairs = []
            for a in range(half_rows):
                for b in range(half_cols):
                    pairs.append((a * col_count + b, (2 * a + u) * col_count + 2 * b + v))
                    pairs.append(
                        (
                            (half_rows + a) * col_count + half_cols + b,
                            (2 * a + 1 - u) * col_count + 2 * b + 1 - v,
                        )
                    )
            received[2 * u + v] = lax.ppermute(messages[2 * u + v], ("row", "col"), pairs)
    quarter = 2 * (row_place % 2) + col_place % 2
    quarter = jnp.where(zoom_start[0] > 0, 3 - quarter, quarter)
    window = jnp.where(
        quarter < 2,
        jnp.where(quarter == 0, received[0], received[1]),
        jnp.where(quarter == 2, received[2], received[3]),
    )

    parts = refine_first.reshape(3, channels, 3, 2 * channels)
    window_weights = parts[..., :channels].reshape(stacked, stacked)
    fine_parts = parts[..., channels:]
    row_terms, col_terms = call(
        fine_kernel,
        (struct((rows + 32, channels, 128), f32), struct((2, 3, channels, 128), f32)),
        [pltpu.VMEM((2, channels, 128), f32)],
        (1 << 28, 4 << 20),
        "fine",
    )(
        pos,
        fine_parts.transpose(2, 1, 0, 3).reshape(stacked, stacked),
        fine_parts.reshape(stacked, stacked),
        refine_bias[0][:, None],
        feats,
    )

    coarse = jnp.transpose(coarse, (1, 0, 2))
    second_weights = refine_second.reshape(stacked, stacked)
    second_bias = refine_bias[1][:, None]
    window, coarse, row_terms, col_terms, window_weights, second_weights, second_bias = (
        lax.optimization_barrier(
            (window, coarse, row_terms, col_terms, window_weights, second_weights, second_bias)
        )
    )
    window_rim = 6
    row_a, row_b = row_swap(window, window_rim)
    pairs = rows // 4 + 2 * window_rim
    pack = struct((pairs // 4, channels, 128))
    col_a, col_b = col_swap(
        *call(strip_pack_window, (pack, pack), [], (1 << 20, 1 << 20), "window_strips")(
            pos, window, row_a, row_b
        )
    )
    fine_rows = rows // 2 + 16
    refined = call(
        refine_kernel,
        struct((rows, channels, cols)),
        [
            pltpu.VMEM((pairs, stacked, 256), bf16),
            pltpu.VMEM((fine_rows, stacked, 256), bf16),
            pltpu.VMEM((pairs, stacked, 256), f32),
            pltpu.VMEM((fine_rows, stacked, 256), f32),
        ],
        (3 << 30, 6 << 20),
        "refine",
    )(
        pos,
        window_weights,
        second_weights,
        second_bias,
        window, row_a, row_b, col_a, col_b, row_terms, col_terms,
    )
    return coarse, jnp.transpose(refined, (1, 0, 2))


def solution(mesh):
    return jax.shard_map(
        per_device,
        mesh=mesh,
        in_specs=(
            P(None, ("row", "col")),
            P(None, ("row", "col")),
            P(None, "row", "col"),
            P(),
            P(),
            P(),
            P(),
            P(),
            P(),
        ),
        out_specs=(P(None, "row", "col"), P(None, "row", "col")),
        check_vma=False,
    )
```

time: 147 us -> 111 us (0.76)
  the two profiles are of different devices: /device:TPU:13 before, /device:TPU:10 now
where the time goes in v2:
time: 111 us; the launch traced here: 110 us
  Pallas kernels  50.1 us (45%)
  starting transfers between devices  32.8 us (30%)
  local copies, waits for them, and re-layouts  17.9 us (16%)
  waiting for transfers between devices  7.18 us (6%)
    pallas_call x7, Pallas kernels, run(): pl.pallas_call(body, out_shape=outs, in_specs=[SMEM] + [VMEM] * (len(args...  50.1 us
    ppermute x4, starting transfers between devices, per_device(): lax.ppermute(messages[2 * u + v], ('row', 'col'), pairs)  14.2 us
    unnamed x31, local copies, waits for them, and re-layouts  10.9 us
    ppermute x4, starting transfers between devices, col_swap(): return (lax.ppermute(a, 'col', first), lax.ppermute(b, 'col', second))  6.8 us
    all_to_all x1, starting transfers between devices, per_device(): lax.all_to_all(spread, ('row', 'col'), split_axis=0, concat_axis=0, tiled...  6.02 us
    ppermute x2, waiting for transfers between devices, row_swap(): lax.ppermute(jnp.where(odd_row, bottom, top), 'row', second)  4.74 us
    ppermute x2, starting transfers between devices, row_swap(): lax.ppermute(jnp.where(odd_row, bottom, top), 'row', second)  4.29 us
    ppermute x4, waiting for transfers between devices, col_swap(): return (lax.ppermute(a, 'col', first), lax.ppermute(b, 'col', second))  2.42 us
  transfers between devices with their start and end apart: 13, of which 4 were waited for; matrix products, arithmetic and copies ran while one was open for 10% of the time, Pallas kernels for 18%

profile of v2, /device:TPU:10, one launch (start us, length us, event | category | flops | bytes accessed | tf_op | source)
XLA Modules:
  0.0 109.8 jit_solution(13666492083425984239)
XLA Ops:
  0.6 0.0 copy-start.8
  0.6 0.0 copy-start.13
  0.7 0.0 copy-start.7
  0.7 0.0 copy-start.2
  0.7 0.8 maximum_bitcast_fusion
  1.5 0.7 broadcast_in_dim.10
  2.2 6.0 %all-to-all-start = ((bf16[32,16,128]{2,1,0:T(8,128)(2,1)}), bf16[32,16,128]{2,1,0:T(8,128)(2,1)S(1)}, u32[]{:S(2)}, u32[]{:S(2)}) async-start(bf16[32,16,128]{2,1,0:T(8,128)(2,1)} %broadcast_in_dim.10), calls=%async_computation | async-start | bytes 262144 | tf_op jit(solution)/shard_map/all_to_all | solution.py:440
  8.2 1.9 %copy.30 = bf16[64,64,128]{2,0,1:T(8,128)(2,1)S(1)} copy(bf16[64,64,128]{2,1,0:T(8,128)(2,1)} %param.11) | data formatting | bytes 2097152 | tf_op args[2]
  10.1 0.0 copy-start
  10.2 2.2 %collective-permute-start.1 = (bf16[6,64,128]{2,1,0:T(8,128)(2,1)S(1)}, bf16[6,64,128]{2,1,0:T(8,128)(2,1)S(1)}, u32[]{:S(2)}, u32[]{:S(2)}) collective-permute-start(bf16[6,64,128]{2,1,0:T(8,128)(2,1)S(1)} %get-tuple-element.42), channel_id=1, source_target_pairs={{4,8},{12,16},{20,24},{8,4},{16,12},{24,20},{5,9},{13,17},{21,25},... | collective-permute-start | bytes 294920 | tf_op jit(solution)/shard_map/ppermute | solution.py:448
  12.4 1.4 %collective-permute-start = (bf16[6,64,128]{2,1,0:T(8,128)(2,1)S(1)}, bf16[6,64,128]{2,1,0:T(8,128)(2,1)S(1)}, u32[]{:S(2)}, u32[]{:S(2)}) collective-permute-start(bf16[6,64,128]{2,1,0:T(8,128)(2,1)S(1)} %get-tuple-element.43), channel_id=1, source_target_pairs={{0,4},{4,0},{8,12},{12,8},{16,20},{20,16},{24,28},{28,24},{1,5},{5... | collective-permute-start | bytes 294920 | tf_op jit(solution)/shard_map/ppermute | solution.py:447
  13.7 0.6 stack.11.pos
  14.3 0.0 all-to-all-done
  14.3 0.8 copy.20
  15.1 1.0 collective-permute-done.1.row_b
  16.1 0.0 collective-permute-done.row_a
  16.1 0.0 copy-done
  16.1 0.6 copy-done.3
  16.7 0.0 copy-done.4
  16.8 3.5 %pair.1 = (bf16[76,64,128]{2,1,0:T(8,128)(2,1)}, bf16[5,64,128]{2,1,0:T(8,128)(2,1)}, bf16[5,64,128]{2,1,0:T(8,128)(2,1)}) custom-call(s32[5]{0:T(128)} %stack.11.pos, bf16[128,512]{1,0:T(8,128)(2,1)} %bitcast.26, bf16[64,64,128]{2,1,0:T(8,128)(2,1)} %bitcast.23, bf16[6,64,128]{2,1,0:T(8,128)(2,1)} %copy-done.4, bf16[6,64,128]{2,1,0:T(8,128)(2,1)} %copy-done.3), custom_call_target="tpu_custom_call" | custom-call | flops 268435456 | bytes 4194304 | tf_op jit(solution)/shard_map/pair/pallas_call | solution.py:19
  20.3 0.8 collective-permute-start.2
  21.1 4.1 %collective-permute-start.3 = (bf16[5,64,128]{2,1,0:T(8,128)(2,1)}, bf16[5,64,128]{2,1,0:T(8,128)(2,1)S(1)}, u32[]{:S(2)}, u32[]{:S(2)}) collective-permute-start(bf16[5,64,128]{2,1,0:T(8,128)(2,1)} %get-tuple-element.22), channel_id=1, source_target_pairs={{1,2},{2,1},{5,6},{6,5},{9,10},{10,9},{13,14},{14,13},{17,18},{18,... | collective-permute-start | bytes 245768 | tf_op jit(solution)/shard_map/ppermute | solution.py:453
  25.2 0.0 copy-done.8
  25.3 0.7 copy.25.bias
  26.0 0.0 copy-done.7
  26.0 0.7 copy.22.bias
  26.8 0.0 collective-permute-done.2.col_a
  26.8 0.0 copy-start.11
  26.8 1.0 collective-permute-done.3.col_b
  27.9 0.6 copy-done.12
  28.5 11.3 %tile1.1 = (bf16[16,64,128]{2,1,0:T(8,128)(2,1)}, bf16[16,64,128]{2,1,0:T(8,128)(2,1)}) custom-call(s32[5]{0:T(128)} %stack.11.pos, bf16[2,192,192]{2,1,0:T(8,128)(2,1)} %bitcast.30, f32[2,64,1]{2,1,0:T(8,128)} %copy.22.bias, bf16[76,64,128]{2,1,0:T(8,128)(2,1)} %get-tuple-element.20.pair, bf16[5,64,128]{2,1,0:T(8,128)(2,1)} %copy-done.11, ...), custom_call_target="tpu_custom_call" | custom-call | flops 3221225472 | bytes 3145728 | tf_op jit(solution)/shard_map/tile1/pallas_call | solution.py:19
  39.8 3.7 %collective-permute-start.5 = (bf16[16,64,128]{2,1,0:T(8,128)(2,1)}, bf16[16,64,128]{2,1,0:T(8,128)(2,1)S(1)}, u32[]{:S(2)}, u32[]{:S(2)}) collective-permute-start(bf16[16,64,128]{2,1,0:T(8,128)(2,1)} %get-tuple-element.24.m01), channel_id=1, source_target_pairs={{0,1},{18,4},{1,3},{19,6},{4,9},{22,12},{5,11},{23,14},{8,17},{26,... | collective-permute-start | bytes 786440 | tf_op jit(solution)/shard_map/ppermute | solution.py:511
  43.5 5.4 %collective-permute-start.7 = (bf16[16,64,128]{2,1,0:T(8,128)(2,1)}, bf16[16,64,128]{2,1,0:T(8,128)(2,1)S(1)}, u32[]{:S(2)}, u32[]{:S(2)}) collective-permute-start(bf16[16,64,128]{2,1,0:T(8,128)(2,1)} %get-tuple-element.26.m11), channel_id=1, source_target_pairs={{0,5},{18,0},{1,7},{19,2},{4,13},{22,8},{5,15},{23,10},{8,21},{26,... | collective-permute-start | bytes 786440 | tf_op jit(solution)/shard_map/ppermute | solution.py:511
  48.9 11.3 %tile0.1 = (bf16[16,64,128]{2,1,0:T(8,128)(2,1)}, bf16[16,64,128]{2,1,0:T(8,128)(2,1)}) custom-call(s32[5]{0:T(128)} %stack.11.pos, bf16[2,192,192]{2,1,0:T(8,128)(2,1)} %bitcast.31, f32[2,64,1]{2,1,0:T(8,128)} %copy.22.bias, bf16[76,64,128]{2,1,0:T(8,128)(2,1)} %get-tuple-element.20.pair, bf16[5,64,128]{2,1,0:T(8,128)(2,1)} %copy-done.11, ...), custom_call_target="tpu_custom_call" | custom-call | flops 3221225472 | bytes 3145728 | tf_op jit(solution)/shard_map/tile0/pallas_call | solution.py:19
  60.2 1.5 %collective-permute-start.4 = (bf16[16,64,128]{2,1,0:T(8,128)(2,1)}, bf16[16,64,128]{2,1,0:T(8,128)(2,1)S(1)}, u32[]{:S(2)}, u32[]{:S(2)}) collective-permute-start(bf16[16,64,128]{2,1,0:T(8,128)(2,1)} %get-tuple-element.23.m00), channel_id=1, source_target_pairs={{0,0},{18,5},{1,2},{19,7},{4,8},{22,13},{5,10},{23,15},{8,16},{26,... | collective-permute-start | bytes 786440 | tf_op jit(solution)/shard_map/ppermute | solution.py:511
  61.7 3.6 %collective-permute-start.6 = (bf16[16,64,128]{2,1,0:T(8,128)(2,1)}, bf16[16,64,128]{2,1,0:T(8,128)(2,1)S(1)}, u32[]{:S(2)}, u32[]{:S(2)}) collective-permute-start(bf16[16,64,128]{2,1,0:T(8,128)(2,1)} %get-tuple-element.25.m10), channel_id=1, source_target_pairs={{0,4},{18,1},{1,6},{19,3},{4,12},{22,9},{5,14},{23,11},{8,20},{26,... | collective-permute-start | bytes 786440 | tf_op jit(solution)/shard_map/ppermute | solution.py:511
  65.4 0.2 fusion
  65.6 0.8 reshape.33.weights
  66.4 0.8 reshape.32.col_weights
  67.2 0.2 copy.24
  67.3 0.8 reshape.31.row_weights
  68.2 5.2 %fine.1 = (f32[96,64,128]{2,1,0:T(8,128)}, f32[2,3,64,128]{3,2,1,0:T(8,128)}) custom-call(s32[5]{0:T(128)} %stack.11.pos, bf16[192,192]{1,0:T(8,128)(2,1)} %reshape.31.row_weights, bf16[192,192]{1,0:T(8,128)(2,1)} %reshape.32.col_weights, f32[64,1]{1,0:T(8,128)} %copy.25.bias, bf16[128,512]{1,0:T(8,128)(2,1)} %bitcast.27), custom_call_target="tpu_custom_call" | custom-call | flops 268435456 | bytes 4194304 | tf_op jit(solution)/shard_map/fine/pallas_call | solution.py:19
  73.4 3.0 %assemble.1 = bf16[64,64,128]{2,1,0:T(8,128)(2,1)} custom-call(s32[5]{0:T(128)} %stack.11.pos, bf16[16,64,128]{2,1,0:T(8,128)(2,1)} %get-tuple-element.23.m00, bf16[16,64,128]{2,1,0:T(8,128)(2,1)} %get-tuple-element.24.m01, bf16[16,64,128]{2,1,0:T(8,128)(2,1)} %get-tuple-element.25.m10, bf16[16,64,128]{2,1,0:T(8,128)(2,1)} %get-tuple-element.26.m11), custom_call_target="tpu_custom_call" | custom-call | flops 1048576 | bytes 2097152 | tf_op jit(solution)/shard_map/assemble/pallas_call | solution.py:19
  76.4 0.0 collective-permute-done.5
  76.4 0.0 collective-permute-done.7
  76.4 0.0 collective-permute-done.4
  76.4 0.0 collective-permute-done.6
  76.4 0.1 select_select_fusion.center
  76.5 2.1 %collective-permute-start.9 = (bf16[6,64,128]{2,1,0:T(8,128)(2,1)S(1)}, bf16[6,64,128]{2,1,0:T(8,128)(2,1)S(1)}, u32[]{:S(2)}, u32[]{:S(2)}) collective-permute-start(bf16[6,64,128]{2,1,0:T(8,128)(2,1)S(1)} %get-tuple-element.44), channel_id=1, source_target_pairs={{4,8},{12,16},{20,24},{8,4},{16,12},{24,20},{5,9},{13,17},{21,25},... | collective-permute-start | bytes 294920 | tf_op jit(solution)/shard_map/ppermute | solution.py:448
  78.6 0.1 collective-permute-start.8
  78.7 3.7 %collective-permute-done.9.row_b = bf16[6,64,128]{2,1,0:T(8,128)(2,1)S(1)} collective-permute-done((bf16[6,64,128]{2,1,0:T(8,128)(2,1)S(1)}, bf16[6,64,128]{2,1,0:T(8,128)(2,1)S(1)}, u32[]{:S(2)}, u32[]{:S(2)}) %collective-permute-start.9) | collective-permute-done | bytes 98336 | tf_op jit(solution)/shard_map/ppermute | solution.py:448
  82.5 0.0 collective-permute-done.8.row_a
  82.5 0.6 copy-done.5
  83.1 0.6 copy-done.6
  83.8 2.1 %window_strips.1 = (bf16[7,64,128]{2,1,0:T(8,128)(2,1)}, bf16[7,64,128]{2,1,0:T(8,128)(2,1)}) custom-call(s32[5]{0:T(128)} %stack.11.pos, bf16[16,64,128]{2,1,0:T(8,128)(2,1)} %copy-done.1, bf16[6,64,128]{2,1,0:T(8,128)(2,1)} %copy-done.6, bf16[6,64,128]{2,1,0:T(8,128)(2,1)} %copy-done.5), custom_call_target="tpu_custom_call" | custom-call | flops 1048576 | bytes 1048576 | tf_op jit(solution)/shard_map/window_strips/pallas_call | solution.py:19
  85.9 0.0 collective-permute-start.10
  85.9 1.9 %collective-permute-start.11 = (bf16[7,64,128]{2,1,0:T(8,128)(2,1)}, bf16[7,64,128]{2,1,0:T(8,128)(2,1)S(1)}, u32[]{:S(2)}, u32[]{:S(2)}) collective-permute-start(bf16[7,64,128]{2,1,0:T(8,128)(2,1)} %get-tuple-element.35), channel_id=1, source_target_pairs={{1,2},{2,1},{5,6},{6,5},{9,10},{10,9},{13,14},{14,13},{17,18},{18,... | collective-permute-start | bytes 344072 | tf_op jit(solution)/shard_map/ppermute | solution.py:453
  87.8 2.9 %copy.27 = bf16[64,64,128]{2,1,0:T(8,128)(2,1)} copy(bf16[64,64,128]{2,0,1:T(8,128)(2,1)} %bitcast.24) | data formatting | bytes 2097152
  90.7 0.7 copy.26.bias2
  91.4 0.0 collective-permute-done.10.col_a
  91.4 1.4 %collective-permute-done.11.col_b = bf16[7,64,128]{2,1,0:T(8,128)(2,1)S(1)} collective-permute-done((bf16[7,64,128]{2,1,0:T(8,128)(2,1)}, bf16[7,64,128]{2,1,0:T(8,128)(2,1)S(1)}, u32[]{:S(2)}, u32[]{:S(2)}) %collective-permute-start.11) | collective-permute-done | bytes 114720 | tf_op jit(solution)/shard_map/ppermute | solution.py:453
  92.8 0.6 copy-done.10
  93.4 13.6 %refine.1 = bf16[64,64,128]{2,1,0:T(8,128)(2,1)} custom-call(s32[5]{0:T(128)} %stack.11.pos, bf16[192,192]{1,0:T(8,128)(2,1)} %reshape.33.weights, bf16[192,192]{1,0:T(8,128)(2,1)} %bitcast.32, f32[64,1]{1,0:T(8,128)} %copy.26.bias2, bf16[16,64,128]{2,1,0:T(8,128)(2,1)} %copy-done.1, bf16[6,64,128]{2,1,0:T(8,128)(2,1)} %copy-done.6, ...), custom_call_target="tpu_custom_call" | custom-call | flops 3221225472 | bytes 6291456 | tf_op jit(solution)/shard_map/refine/pallas_call | solution.py:19
  107.0 2.9 %copy.28 = bf16[64,64,128]{2,1,0:T(8,128)(2,1)} copy(bf16[64,64,128]{2,0,1:T(8,128)(2,1)} %bitcast.25) | data formatting | bytes 2097152
  (17 shorter events, 0.1 us)
Async XLA Ops:
  0.6 24.6 %copy-start.8 = (f32[2,64]{1,0:T(2,128)S(1)}, f32[2,64]{1,0:T(2,128)}, u32[]{:S(2)}) copy-start(f32[2,64]{1,0:T(2,128)} %param.17) | copy-start | bytes 1540
  0.6 24.6 %copy-start.13 = (s32[2]{0:T(128)S(1)}, s32[2]{0:T(128)}, u32[]{:S(2)}) copy-start(s32[2]{0:T(128)} %param.12) | copy-start | bytes 28
  0.7 25.4 %copy-start.7 = (f32[2,64]{1,0:T(2,128)S(1)}, f32[2,64]{1,0:T(2,128)}, u32[]{:S(2)}) copy-start(f32[2,64]{1,0:T(2,128)} %param.14) | copy-start | bytes 1540
  0.7 26.1 %copy-start.2 = (bf16[3,64,384]{2,1,0:T(8,128)(2,1)S(1)}, bf16[3,64,384]{2,1,0:T(8,128)(2,1)}, u32[]{:S(2)}) copy-start(bf16[3,64,384]{2,1,0:T(8,128)(2,1)} %param.15) | copy-start | bytes 442372
  2.2 12.2 %all-to-all-start = ((bf16[32,16,128]{2,1,0:T(8,128)(2,1)}), bf16[32,16,128]{2,1,0:T(8,128)(2,1)S(1)}, u32[]{:S(2)}, u32[]{:S(2)}) async-start(bf16[32,16,128]{2,1,0:T(8,128)(2,1)} %broadcast_in_dim.10), calls=%async_computation | async-start | bytes 262144 | tf_op jit(solution)/shard_map/all_to_all | solution.py:440
  10.1 6.0 %copy-start = (bf16[64,64,128]{2,0,1:T(8,128)(2,1)}, bf16[64,64,128]{2,0,1:T(8,128)(2,1)S(1)}, u32[]{:S(2)}) copy-start(bf16[64,64,128]{2,0,1:T(8,128)(2,1)S(1)} %copy.30) | copy-start | bytes 3145732
  10.2 5.9 %collective-permute-start.1 = (bf16[6,64,128]{2,1,0:T(8,128)(2,1)S(1)}, bf16[6,64,128]{2,1,0:T(8,128)(2,1)S(1)}, u32[]{:S(2)}, u32[]{:S(2)}) collective-permute-start(bf16[6,64,128]{2,1,0:T(8,128)(2,1)S(1)} %get-tuple-element.42), channel_id=1, source_target_pairs={{4,8},{12,16},{20,24},{8,4},{16,12},{24,20},{5,9},{13,17},{21,25},... | collective-permute-start | bytes 294920 | tf_op jit(solution)/shard_map/ppermute | solution.py:448
  12.4 3.7 %collective-permute-start = (bf16[6,64,128]{2,1,0:T(8,128)(2,1)S(1)}, bf16[6,64,128]{2,1,0:T(8,128)(2,1)S(1)}, u32[]{:S(2)}, u32[]{:S(2)}) collective-permute-start(bf16[6,64,128]{2,1,0:T(8,128)(2,1)S(1)} %get-tuple-element.43), channel_id=1, source_target_pairs={{0,4},{4,0},{8,12},{12,8},{16,20},{20,16},{24,28},{28,24},{1,5},{5... | collective-permute-start | bytes 294920 | tf_op jit(solution)/shard_map/ppermute | solution.py:447
  16.1 0.6 copy-start.3
  16.1 0.7 copy-start.4
  20.3 6.5 %collective-permute-start.2 = (bf16[5,64,128]{2,1,0:T(8,128)(2,1)}, bf16[5,64,128]{2,1,0:T(8,128)(2,1)S(1)}, u32[]{:S(2)}, u32[]{:S(2)}) collective-permute-start(bf16[5,64,128]{2,1,0:T(8,128)(2,1)} %get-tuple-element.21), channel_id=1, source_target_pairs={{0,1},{1,0},{2,3},{3,2},{4,5},{5,4},{6,7},{7,6},{8,9},{9,8},{10,11... | collective-permute-start | bytes 245768 | tf_op jit(solution)/shard_map/ppermute | solution.py:453
  21.1 6.7 %collective-permute-start.3 = (bf16[5,64,128]{2,1,0:T(8,128)(2,1)}, bf16[5,64,128]{2,1,0:T(8,128)(2,1)S(1)}, u32[]{:S(2)}, u32[]{:S(2)}) collective-permute-start(bf16[5,64,128]{2,1,0:T(8,128)(2,1)} %get-tuple-element.22), channel_id=1, source_target_pairs={{1,2},{2,1},{5,6},{6,5},{9,10},{10,9},{13,14},{14,13},{17,18},{18,... | collective-permute-start | bytes 245768 | tf_op jit(solution)/shard_map/ppermute | solution.py:453
  26.8 1.0 copy-start.11
  27.9 0.6 copy-start.12
  39.8 36.6 %collective-permute-start.5 = (bf16[16,64,128]{2,1,0:T(8,128)(2,1)}, bf16[16,64,128]{2,1,0:T(8,128)(2,1)S(1)}, u32[]{:S(2)}, u32[]{:S(2)}) collective-permute-start(bf16[16,64,128]{2,1,0:T(8,128)(2,1)} %get-tuple-element.24.m01), channel_id=1, source_target_pairs={{0,1},{18,4},{1,3},{19,6},{4,9},{22,12},{5,11},{23,14},{8,17},{26,... | collective-permute-start | bytes 786440 | tf_op jit(solution)/shard_map/ppermute | solution.py:511
  43.5 32.9 %collective-permute-start.7 = (bf16[16,64,128]{2,1,0:T(8,128)(2,1)}, bf16[16,64,128]{2,1,0:T(8,128)(2,1)S(1)}, u32[]{:S(2)}, u32[]{:S(2)}) collective-permute-start(bf16[16,64,128]{2,1,0:T(8,128)(2,1)} %get-tuple-element.26.m11), channel_id=1, source_target_pairs={{0,5},{18,0},{1,7},{19,2},{4,13},{22,8},{5,15},{23,10},{8,21},{26,... | collective-permute-start | bytes 786440 | tf_op jit(solution)/shard_map/ppermute | solution.py:511
  60.2 16.2 %collective-permute-start.4 = (bf16[16,64,128]{2,1,0:T(8,128)(2,1)}, bf16[16,64,128]{2,1,0:T(8,128)(2,1)S(1)}, u32[]{:S(2)}, u32[]{:S(2)}) collective-permute-start(bf16[16,64,128]{2,1,0:T(8,128)(2,1)} %get-tuple-element.23.m00), channel_id=1, source_target_pairs={{0,0},{18,5},{1,2},{19,7},{4,8},{22,13},{5,10},{23,15},{8,16},{26,... | collective-permute-start | bytes 786440 | tf_op jit(solution)/shard_map/ppermute | solution.py:511
  61.7 14.7 %collective-permute-start.6 = (bf16[16,64,128]{2,1,0:T(8,128)(2,1)}, bf16[16,64,128]{2,1,0:T(8,128)(2,1)S(1)}, u32[]{:S(2)}, u32[]{:S(2)}) collective-permute-start(bf16[16,64,128]{2,1,0:T(8,128)(2,1)} %get-tuple-element.25.m10), channel_id=1, source_target_pairs={{0,4},{18,1},{1,6},{19,3},{4,12},{22,9},{5,14},{23,11},{8,20},{26,... | collective-permute-start | bytes 786440 | tf_op jit(solution)/shard_map/ppermute | solution.py:511
  76.5 6.0 %copy-start.1 = (bf16[16,64,128]{2,1,0:T(8,128)(2,1)}, bf16[16,64,128]{2,1,0:T(8,128)(2,1)S(1)}, u32[]{:S(2)}) copy-start(bf16[16,64,128]{2,1,0:T(8,128)(2,1)S(1)} %select_select_fusion.center) | copy-start | bytes 786436
  76.5 5.9 %collective-permute-start.9 = (bf16[6,64,128]{2,1,0:T(8,128)(2,1)S(1)}, bf16[6,64,128]{2,1,0:T(8,128)(2,1)S(1)}, u32[]{:S(2)}, u32[]{:S(2)}) collective-permute-start(bf16[6,64,128]{2,1,0:T(8,128)(2,1)S(1)} %get-tuple-element.44), channel_id=1, source_target_pairs={{4,8},{12,16},{20,24},{8,4},{16,12},{24,20},{5,9},{13,17},{21,25},... | collective-permute-start | bytes 294920 | tf_op jit(solution)/shard_map/ppermute | solution.py:448
  78.6 3.8 %collective-permute-start.8 = (bf16[6,64,128]{2,1,0:T(8,128)(2,1)S(1)}, bf16[6,64,128]{2,1,0:T(8,128)(2,1)S(1)}, u32[]{:S(2)}, u32[]{:S(2)}) collective-permute-start(bf16[6,64,128]{2,1,0:T(8,128)(2,1)S(1)} %get-tuple-element.45), channel_id=1, source_target_pairs={{0,4},{4,0},{8,12},{12,8},{16,20},{20,16},{24,28},{28,24},{1,5},{5... | collective-permute-start | bytes 294920 | tf_op jit(solution)/shard_map/ppermute | solution.py:447
  82.5 0.6 copy-start.5
  83.1 0.6 copy-start.6
  85.9 5.5 %collective-permute-start.10 = (bf16[7,64,128]{2,1,0:T(8,128)(2,1)}, bf16[7,64,128]{2,1,0:T(8,128)(2,1)S(1)}, u32[]{:S(2)}, u32[]{:S(2)}) collective-permute-start(bf16[7,64,128]{2,1,0:T(8,128)(2,1)} %get-tuple-element.34), channel_id=1, source_target_pairs={{0,1},{1,0},{2,3},{3,2},{4,5},{5,4},{6,7},{7,6},{8,9},{9,8},{10,11... | collective-permute-start | bytes 344072 | tf_op jit(solution)/shard_map/ppermute | solution.py:453
  85.9 6.9 %collective-permute-start.11 = (bf16[7,64,128]{2,1,0:T(8,128)(2,1)}, bf16[7,64,128]{2,1,0:T(8,128)(2,1)S(1)}, u32[]{:S(2)}, u32[]{:S(2)}) collective-permute-start(bf16[7,64,128]{2,1,0:T(8,128)(2,1)} %get-tuple-element.35), channel_id=1, source_target_pairs={{1,2},{2,1},{5,6},{6,5},{9,10},{10,9},{13,14},{14,13},{17,18},{18,... | collective-permute-start | bytes 344072 | tf_op jit(solution)/shard_map/ppermute | solution.py:453
  91.4 1.4 %copy-start.9 = (bf16[7,64,128]{2,1,0:T(8,128)(2,1)}, bf16[7,64,128]{2,1,0:T(8,128)(2,1)S(1)}, u32[]{:S(2)}) copy-start(bf16[7,64,128]{2,1,0:T(8,128)(2,1)S(1)} %collective-permute-done.10.col_a) | copy-start | bytes 344068
  92.8 0.6 copy-start.10

commit v3 on v2

--- a/solution.py
+++ b/solution.py
@@ -22,7 +22,7 @@
             in_specs=[SMEM] + [VMEM] * (len(args) - 1),
             out_specs=jax.tree.map(lambda _: VMEM, outs),
             scratch_shapes=scratch,
-            compiler_params=pltpu.CompilerParams(vmem_limit_bytes=56 << 20),
+            compiler_params=pltpu.CompilerParams(vmem_limit_bytes=44 << 20),
             cost_estimate=pl.CostEstimate(flops=flops, bytes_accessed=moved, transcendentals=0),
             name=name,
         )(*args)
@@ -246,20 +246,26 @@
     half = width // 2
     upper = 2 * pos[0] < pos[4] // pos[2]
     low = lanes((channels, width)) < half
-    for u in range(2):
-
-        def pair(p, carry, u=u):
+
+    def chunk(c, carry):
+        u = c * 8 // quarter
+        rows = []
+        for i in range(8):
+            p = c * 8 % quarter + i
             sides = [
-                jnp.where(upper, (m00, m01, m10, m11)[2 * u + v][p], (m11, m10, m01, m00)[2 * u + v][p])
+                jnp.where(
+                    upper, (m00, m01, m10, m11)[2 * u + v][p], (m11, m10, m01, m00)[2 * u + v][p]
+                )
                 for v in range(2)
             ]
             left, right = [side.astype(f32) for side in sides]
-            at = 2 * (quarter * u + p)
-            coarse[at] = jnp.where(low, left, roll(right, half)).astype(bf16)
-            coarse[at + 1] = jnp.where(low, roll(left, half), right).astype(bf16)
-            return carry
-
-        lax.fori_loop(0, quarter, pair, 0, unroll=4)
+            rows.append(jnp.where(low, left, roll(right, half)).astype(bf16))
+            rows.append(jnp.where(low, roll(left, half), right).astype(bf16))
+        coarse[:, 16 * c : 16 * c + 16, :] = jnp.swapaxes(jnp.stack(rows, axis=0), 0, 1)
+        return carry
+
+    for c in range(quarter // 4):
+        chunk(c, 0)
 
 
 def strip_pack_window(pos, center, row_a, row_b, out_a, out_b):
@@ -408,15 +414,18 @@
     source, target = source_and_target(128, 128)
     weave = one_hot(2 * (source % 64) + source // 64 == target)
 
-    def produce(p, carry):
-        value = jnp.maximum(combine(products_h, p, 8) + b2, 0.0).astype(bf16)
-        both = jnp.concatenate([value[:, :128], value[:, 128:]], axis=0)
-        both = dot(both, weave).astype(bf16)
-        refined[2 * p] = both[:channels]
-        refined[2 * p + 1] = both[channels:]
+    def produce(c, carry):
+        rows = []
+        for i in range(8):
+            value = jnp.maximum(combine(products_h, 8 * c + i, 8) + b2, 0.0).astype(bf16)
+            both = jnp.concatenate([value[:, :128], value[:, 128:]], axis=0)
+            both = dot(both, weave).astype(bf16)
+            rows += [both[:channels], both[channels:]]
+        at = pl.multiple_of(16 * c, 16)
+        refined[:, pl.ds(at, 16), :] = jnp.swapaxes(jnp.stack(rows, axis=0), 0, 1)
         return carry
 
-    lax.fori_loop(0, 2 * pairs, produce, 0, unroll=8)
+    lax.fori_loop(0, pairs // 4, produce, 0)
 
 
 def per_device(
@@ -491,7 +500,7 @@
     ]
     messages = [halves[v][u] for u in range(2) for v in range(2)]
     coarse = call(
-        assemble_kernel, struct((rows, channels, cols)), [], (1 << 20, 2 << 20), "assemble"
+        assemble_kernel, struct((channels, rows, cols)), [], (1 << 20, 2 << 20), "assemble"
     )(pos, *messages)
 
     half_rows, half_cols = row_count // 2, col_count // 2
@@ -534,7 +543,6 @@
         feats,
     )
 
-    coarse = jnp.transpose(coarse, (1, 0, 2))
     second_weights = refine_second.reshape(stacked, stacked)
     second_bias = refine_bias[1][:, None]
     window, coarse, row_terms, col_terms, window_weights, second_weights, second_bias = (
@@ -554,7 +562,7 @@
     fine_rows = rows // 2 + 16
     refined = call(
         refine_kernel,
-        struct((rows, channels, cols)),
+        struct((channels, rows, cols)),
         [
             pltpu.VMEM((pairs, stacked, 256), bf16),
             pltpu.VMEM((fine_rows, stacked, 256), bf16),
@@ -570,7 +578,7 @@
         second_bias,
         window, row_a, row_b, col_a, col_b, row_terms, col_terms,
     )
-    return coarse, jnp.transpose(refined, (1, 0, 2))
+    return coarse, refined
 
 
 def solution(mesh):

time: 111 us -> 97.9 us (0.88)
  local copies, waits for them, and re-layouts: 17.9 us -> 5.91 us
  Pallas kernels: 50.1 us -> 39.5 us
  waiting for transfers between devices: 7.18 us -> 14.8 us
  starting transfers between devices: 32.8 us -> 34.4 us
    pallas_call x7, Pallas kernels: 50.1 us -> 39.5 us  [run(): pl.pallas_call(body, out_shape=outs, in_specs=[SMEM] + [VMEM] * (len(args...]
    unnamed x31 -> x17, local copies, waits for them, and re-layouts: 10.9 us -> 3.83 us
    ppermute x4, waiting for transfers between devices: 2.42 us -> 6.74 us  [col_swap(): return (lax.ppermute(a, 'col', first), lax.ppermute(b, 'col', second))]
    ppermute x4, waiting for transfers between devices: 0.01 us -> 1.99 us  [per_device(): lax.ppermute(messages[2 * u + v], ('row', 'col'), pairs)]
    ppermute x4, starting transfers between devices: 14.2 us -> 15.8 us  [per_device(): lax.ppermute(messages[2 * u + v], ('row', 'col'), pairs)]
    ppermute x2, waiting for transfers between devices: 4.74 us -> 5.93 us  [row_swap(): lax.ppermute(jnp.where(odd_row, bottom, top), 'row', second)]
  transfers between devices with their start and end apart: 13 -> 13, of which waited for: 4 -> 7; matrix products, arithmetic and copies ran while one was open for 10% -> 3% of each run, Pallas kernels for 18% -> 15%
where the time goes in v3:
time: 97.9 us; the launch traced here: 97.5 us
  Pallas kernels  39.5 us (40%)
  starting transfers between devices  34.4 us (35%)
  waiting for transfers between devices  14.8 us (15%)
  local copies, waits for them, and re-layouts  5.91 us (6%)
  other arithmetic  1.89 us (2%)
  between operations  0.99 us (1%)
    pallas_call x7, Pallas kernels, run(): pl.pallas_call(body, out_shape=outs, in_specs=[SMEM] + [VMEM] * (len(args...  39.5 us
    ppermute x4, starting transfers between devices, per_device(): lax.ppermute(messages[2 * u + v], ('row', 'col'), pairs)  15.8 us
    ppermute x4, starting transfers between devices, col_swap(): return (lax.ppermute(a, 'col', first), lax.ppermute(b, 'col', second))  6.95 us
    ppermute x4, waiting for transfers between devices, col_swap(): return (lax.ppermute(a, 'col', first), lax.ppermute(b, 'col', second))  6.74 us
    all_to_all x1, starting transfers between devices, per_device(): lax.all_to_all(spread, ('row', 'col'), split_axis=0, concat_axis=0, tiled...  6.02 us
    ppermute x2, waiting for transfers between devices, row_swap(): lax.ppermute(jnp.where(odd_row, bottom, top), 'row', second)  5.93 us
    ppermute x2, starting transfers between devices, row_swap(): lax.ppermute(jnp.where(odd_row, bottom, top), 'row', second)  4.11 us
    unnamed x17, local copies, waits for them, and re-layouts  3.83 us
  transfers between devices with their start and end apart: 13, of which 7 were waited for; matrix products, arithmetic and copies ran while one was open for 3% of the time, Pallas kernels for 15%

profile of v3, /device:TPU:10, one launch (start us, length us, event | category | flops | bytes accessed | tf_op | source)
XLA Modules:
  0.0 97.5 jit_solution(1119339416108999718)
XLA Ops:
  0.6 0.0 copy-start.6
  0.6 0.0 copy-start.7
  0.7 0.0 copy-start.5
  0.7 0.0 copy-start.4
  0.7 0.0 copy-start
  0.7 0.8 maximum_bitcast_fusion
  1.5 0.7 broadcast_in_dim.10
  2.2 6.0 %all-to-all-start = ((bf16[32,16,128]{2,1,0:T(8,128)(2,1)}), bf16[32,16,128]{2,1,0:T(8,128)(2,1)S(1)}, u32[]{:S(2)}, u32[]{:S(2)}) async-start(bf16[32,16,128]{2,1,0:T(8,128)(2,1)} %broadcast_in_dim.10), calls=%async_computation | async-start | bytes 262144 | tf_op jit(solution)/shard_map/all_to_all | solution.py:449
  8.2 1.9 %copy.26 = bf16[64,64,128]{2,0,1:T(8,128)(2,1)S(1)} copy(bf16[64,64,128]{2,1,0:T(8,128)(2,1)} %param.11) | data formatting | bytes 2097152 | tf_op args[2]
  10.2 2.2 %collective-permute-start.1 = (bf16[6,64,128]{2,1,0:T(8,128)(2,1)S(1)}, bf16[6,64,128]{2,1,0:T(8,128)(2,1)S(1)}, u32[]{:S(2)}, u32[]{:S(2)}) collective-permute-start(bf16[6,64,128]{2,1,0:T(8,128)(2,1)S(1)} %get-tuple-element.38), channel_id=1, source_target_pairs={{4,8},{12,16},{20,24},{8,4},{16,12},{24,20},{5,9},{13,17},{21,25},... | collective-permute-start | bytes 294920 | tf_op jit(solution)/shard_map/ppermute | solution.py:457
  12.4 1.4 %collective-permute-start = (bf16[6,64,128]{2,1,0:T(8,128)(2,1)S(1)}, bf16[6,64,128]{2,1,0:T(8,128)(2,1)S(1)}, u32[]{:S(2)}, u32[]{:S(2)}) collective-permute-start(bf16[6,64,128]{2,1,0:T(8,128)(2,1)S(1)} %get-tuple-element.39), channel_id=1, source_target_pairs={{0,4},{4,0},{8,12},{12,8},{16,20},{20,16},{24,28},{28,24},{1,5},{5... | collective-permute-start | bytes 294920 | tf_op jit(solution)/shard_map/ppermute | solution.py:456
  13.7 0.1 stack.11.pos
  13.8 0.2 all-to-all-done
  14.0 0.1 copy.18
  14.1 2.0 %collective-permute-done.1.row_b = bf16[6,64,128]{2,1,0:T(8,128)(2,1)S(1)} collective-permute-done((bf16[6,64,128]{2,1,0:T(8,128)(2,1)S(1)}, bf16[6,64,128]{2,1,0:T(8,128)(2,1)S(1)}, u32[]{:S(2)}, u32[]{:S(2)}) %collective-permute-start.1) | collective-permute-done | bytes 98336 | tf_op jit(solution)/shard_map/ppermute | solution.py:457
  16.1 0.0 collective-permute-done.row_a
  16.1 1.8 %pair.1 = (bf16[76,64,128]{2,1,0:T(8,128)(2,1)S(1)}, bf16[5,64,128]{2,1,0:T(8,128)(2,1)S(1)}, bf16[5,64,128]{2,1,0:T(8,128)(2,1)S(1)}) custom-call(s32[5]{0:T(128)S(1)} %stack.11.pos, bf16[128,512]{1,0:T(8,128)(2,1)S(1)} %bitcast.22, bf16[64,64,128]{2,1,0:T(8,128)(2,1)S(1)} %bitcast.21, bf16[6,64,128]{2,1,0:T(8,128)(2,1)S(1)} %collective-permute-done.row_a, ...), custom_call_target="tpu_custom_call" | custom-call | flops 268435456 | bytes 4194304 | tf_op jit(solution)/shard_map/pair/pallas_call | solution.py:19
  17.9 0.6 collective-permute-start.2
  18.5 4.3 %collective-permute-start.3 = (bf16[5,64,128]{2,1,0:T(8,128)(2,1)S(1)}, bf16[5,64,128]{2,1,0:T(8,128)(2,1)S(1)}, u32[]{:S(2)}, u32[]{:S(2)}) collective-permute-start(bf16[5,64,128]{2,1,0:T(8,128)(2,1)S(1)} %get-tuple-element.22), channel_id=1, source_target_pairs={{1,2},{2,1},{5,6},{6,5},{9,10},{10,9},{13,14},{14,13},{17,18},{18,... | collective-permute-start | bytes 245768 | tf_op jit(solution)/shard_map/ppermute | solution.py:462
  22.8 0.0 copy-done.6
  22.9 0.0 copy-done.7
  22.9 0.1 copy.23.bias
  23.0 0.0 copy-done.5
  23.0 0.1 copy.20.bias
  23.1 0.0 copy-done.4
  23.2 0.0 collective-permute-done.2.col_a
  23.2 2.1 %collective-permute-done.3.col_b = bf16[5,64,128]{2,1,0:T(8,128)(2,1)S(1)} collective-permute-done((bf16[5,64,128]{2,1,0:T(8,128)(2,1)S(1)}, bf16[5,64,128]{2,1,0:T(8,128)(2,1)S(1)}, u32[]{:S(2)}, u32[]{:S(2)}) %collective-permute-start.3) | collective-permute-done | bytes 81952 | tf_op jit(solution)/shard_map/ppermute | solution.py:462
  25.3 0.0 copy-done
  25.3 9.7 %tile1.1 = (bf16[16,64,128]{2,1,0:T(8,128)(2,1)S(1)}, bf16[16,64,128]{2,1,0:T(8,128)(2,1)S(1)}) custom-call(s32[5]{0:T(128)S(1)} %stack.11.pos, bf16[2,192,192]{2,1,0:T(8,128)(2,1)S(1)} %bitcast.24, f32[2,64,1]{2,1,0:T(8,128)S(1)} %copy.20.bias, bf16[76,64,128]{2,1,0:T(8,128)(2,1)S(1)} %get-tuple-element.20.pair, ...), custom_call_target="tpu_custom_call" | custom-call | flops 3221225472 | bytes 3145728 | tf_op jit(solution)/shard_map/tile1/pallas_call | solution.py:19
  35.0 3.7 %collective-permute-start.5 = (bf16[16,64,128]{2,1,0:T(8,128)(2,1)S(1)}, bf16[16,64,128]{2,1,0:T(8,128)(2,1)}, u32[]{:S(2)}, u32[]{:S(2)}) collective-permute-start(bf16[16,64,128]{2,1,0:T(8,128)(2,1)S(1)} %get-tuple-element.24.m01), channel_id=1, source_target_pairs={{0,1},{18,4},{1,3},{19,6},{4,9},{22,12},{5,11},{23,14},{8,17},{26,... | collective-permute-start | bytes 786440 | tf_op jit(solution)/shard_map/ppermute | solution.py:520
  38.7 6.8 %collective-permute-start.7 = (bf16[16,64,128]{2,1,0:T(8,128)(2,1)S(1)}, bf16[16,64,128]{2,1,0:T(8,128)(2,1)}, u32[]{:S(2)}, u32[]{:S(2)}) collective-permute-start(bf16[16,64,128]{2,1,0:T(8,128)(2,1)S(1)} %get-tuple-element.26.m11), channel_id=1, source_target_pairs={{0,5},{18,0},{1,7},{19,2},{4,13},{22,8},{5,15},{23,10},{8,21},{26,... | collective-permute-start | bytes 786440 | tf_op jit(solution)/shard_map/ppermute | solution.py:520
  45.5 9.7 %tile0.1 = (bf16[16,64,128]{2,1,0:T(8,128)(2,1)S(1)}, bf16[16,64,128]{2,1,0:T(8,128)(2,1)S(1)}) custom-call(s32[5]{0:T(128)S(1)} %stack.11.pos, bf16[2,192,192]{2,1,0:T(8,128)(2,1)S(1)} %bitcast.25, f32[2,64,1]{2,1,0:T(8,128)S(1)} %copy.20.bias, bf16[76,64,128]{2,1,0:T(8,128)(2,1)S(1)} %get-tuple-element.20.pair, ...), custom_call_target="tpu_custom_call" | custom-call | flops 3221225472 | bytes 3145728 | tf_op jit(solution)/shard_map/tile0/pallas_call | solution.py:19
  55.1 1.3 %collective-permute-start.4 = (bf16[16,64,128]{2,1,0:T(8,128)(2,1)S(1)}, bf16[16,64,128]{2,1,0:T(8,128)(2,1)S(1)}, u32[]{:S(2)}, u32[]{:S(2)}) collective-permute-start(bf16[16,64,128]{2,1,0:T(8,128)(2,1)S(1)} %get-tuple-element.23.m00), channel_id=1, source_target_pairs={{0,0},{18,5},{1,2},{19,7},{4,8},{22,13},{5,10},{23,15},{8,16},{26,... | collective-permute-start | bytes 786440 | tf_op jit(solution)/shard_map/ppermute | solution.py:520
  56.5 4.0 %collective-permute-start.6 = (bf16[16,64,128]{2,1,0:T(8,128)(2,1)S(1)}, bf16[16,64,128]{2,1,0:T(8,128)(2,1)S(1)}, u32[]{:S(2)}, u32[]{:S(2)}) collective-permute-start(bf16[16,64,128]{2,1,0:T(8,128)(2,1)S(1)} %get-tuple-element.25.m10), channel_id=1, source_target_pairs={{0,4},{18,1},{1,6},{19,3},{4,12},{22,9},{5,14},{23,11},{8,20},{26,... | collective-permute-start | bytes 786440 | tf_op jit(solution)/shard_map/ppermute | solution.py:520
  60.5 0.2 fusion
  60.7 0.2 reshape.33.weights
  60.9 0.0 copy-start.1
  60.9 0.2 reshape.32.col_weights
  61.1 0.2 copy.22
  61.2 0.2 reshape.31.row_weights
  61.4 3.1 %fine.1 = (f32[96,64,128]{2,1,0:T(8,128)S(1)}, f32[2,3,64,128]{3,2,1,0:T(8,128)S(1)}) custom-call(s32[5]{0:T(128)S(1)} %stack.11.pos, bf16[192,192]{1,0:T(8,128)(2,1)S(1)} %reshape.31.row_weights, bf16[192,192]{1,0:T(8,128)(2,1)S(1)} %reshape.32.col_weights, f32[64,1]{1,0:T(8,128)S(1)} %copy.23.bias, bf16[128,512]{1,0:T(8,128)(2,1)S(1)} %bitcast.23), custom_call_target="tpu_custom_call" | custom-call | flops 268435456 | bytes 4194304 | tf_op jit(solution)/shard_map/fine/pallas_call | solution.py:19
  64.5 0.0 copy-start.2
  64.5 2.3 %assemble.1 = bf16[64,64,128]{2,1,0:T(8,128)(2,1)} custom-call(s32[5]{0:T(128)S(1)} %stack.11.pos, bf16[16,64,128]{2,1,0:T(8,128)(2,1)S(1)} %get-tuple-element.23.m00, bf16[16,64,128]{2,1,0:T(8,128)(2,1)S(1)} %get-tuple-element.24.m01, bf16[16,64,128]{2,1,0:T(8,128)(2,1)S(1)} %get-tuple-element.25.m10, bf16[16,64,128]{2,1,0:T(8,128)(2,1)S(1)} %get-tuple-element.26.m11), custom_call_target="tpu_custom_call" | custom-call | flops 1048576 | bytes 2097152 | tf_op jit(solution)/shard_map/assemble/pallas_call | solution.py:19
  66.8 0.0 collective-permute-done.5
  66.8 0.0 collective-permute-done.7
  66.8 0.0 collective-permute-done.4
  66.8 2.0 %collective-permute-done.6 = bf16[16,64,128]{2,1,0:T(8,128)(2,1)S(1)} collective-permute-done((bf16[16,64,128]{2,1,0:T(8,128)(2,1)S(1)}, bf16[16,64,128]{2,1,0:T(8,128)(2,1)S(1)}, u32[]{:S(2)}, u32[]{:S(2)}) %collective-permute-start.6) | collective-permute-done | bytes 262176 | tf_op jit(solution)/shard_map/ppermute | solution.py:520
  68.7 1.0 %select_select_fusion.center = bf16[16,64,128]{2,1,0:T(8,128)(2,1)S(1)} fusion(bf16[16,64,128]{2,1,0:T(8,128)(2,1)S(1)} %collective-permute-done.6, bf16[16,64,128]{2,1,0:T(8,128)(2,1)} %collective-permute-done.7, bf16[16,64,128]{2,1,0:T(8,128)(2,1)S(1)} %collective-permute-done.4, bf16[16,64,128]{2,1,0:T(8,128)(2,1)} %collective-permute-done.5, pred[]{:T(512)S(6)} %eq.15, ...), kind=kLoop, calls=%fused_computation.1 | loop fusion | flops 393216 | bytes 1310723 | tf_op jit(solution)/shard_map/jit(_where)/select_n | solution.py:523
  69.8 1.9 %collective-permute-start.9 = (bf16[6,64,128]{2,1,0:T(8,128)(2,1)S(1)}, bf16[6,64,128]{2,1,0:T(8,128)(2,1)S(1)}, u32[]{:S(2)}, u32[]{:S(2)}) collective-permute-start(bf16[6,64,128]{2,1,0:T(8,128)(2,1)S(1)} %get-tuple-element.40), channel_id=1, source_target_pairs={{4,8},{12,16},{20,24},{8,4},{16,12},{24,20},{5,9},{13,17},{21,25},... | collective-permute-start | bytes 294920 | tf_op jit(solution)/shard_map/ppermute | solution.py:457
  71.7 0.1 collective-permute-start.8
  71.8 3.9 %collective-permute-done.9.row_b = bf16[6,64,128]{2,1,0:T(8,128)(2,1)S(1)} collective-permute-done((bf16[6,64,128]{2,1,0:T(8,128)(2,1)S(1)}, bf16[6,64,128]{2,1,0:T(8,128)(2,1)S(1)}, u32[]{:S(2)}, u32[]{:S(2)}) %collective-permute-start.9) | collective-permute-done | bytes 98336 | tf_op jit(solution)/shard_map/ppermute | solution.py:457
  75.7 0.0 collective-permute-done.8.row_a
  75.7 0.9 window_strips.1
  76.7 0.1 collective-permute-start.10
  76.8 0.0 copy-done.2
  76.8 1.9 %collective-permute-start.11 = (bf16[7,64,128]{2,1,0:T(8,128)(2,1)S(1)}, bf16[7,64,128]{2,1,0:T(8,128)(2,1)S(1)}, u32[]{:S(2)}, u32[]{:S(2)}) collective-permute-start(bf16[7,64,128]{2,1,0:T(8,128)(2,1)S(1)} %get-tuple-element.35), channel_id=1, source_target_pairs={{1,2},{2,1},{5,6},{6,5},{9,10},{10,9},{13,14},{14,13},{17,18},{18,... | collective-permute-start | bytes 344072 | tf_op jit(solution)/shard_map/ppermute | solution.py:462
  78.7 0.1 copy.24.bias2
  78.8 2.7 %collective-permute-done.10.col_a = bf16[7,64,128]{2,1,0:T(8,128)(2,1)S(1)} collective-permute-done((bf16[7,64,128]{2,1,0:T(8,128)(2,1)S(1)}, bf16[7,64,128]{2,1,0:T(8,128)(2,1)S(1)}, u32[]{:S(2)}, u32[]{:S(2)}) %collective-permute-start.10) | collective-permute-done | bytes 114720 | tf_op jit(solution)/shard_map/ppermute | solution.py:462
  81.5 1.9 %collective-permute-done.11.col_b = bf16[7,64,128]{2,1,0:T(8,128)(2,1)S(1)} collective-permute-done((bf16[7,64,128]{2,1,0:T(8,128)(2,1)S(1)}, bf16[7,64,128]{2,1,0:T(8,128)(2,1)S(1)}, u32[]{:S(2)}, u32[]{:S(2)}) %collective-permute-start.11) | collective-permute-done | bytes 114720 | tf_op jit(solution)/shard_map/ppermute | solution.py:462
  83.5 0.0 copy-done.1
  83.5 0.0 copy-start.3
  83.5 1.9 %copy-done.3 = f32[96,64,128]{2,1,0:T(8,128)S(1)} copy-done((f32[96,64,128]{2,1,0:T(8,128)S(1)}, f32[96,64,128]{2,1,0:T(8,128)}, u32[]{:S(2)}) %copy-start.3) | copy-done | bytes 3145752
  85.4 12.1 %refine.1 = bf16[64,64,128]{2,1,0:T(8,128)(2,1)} custom-call(s32[5]{0:T(128)S(1)} %stack.11.pos, bf16[192,192]{1,0:T(8,128)(2,1)S(1)} %reshape.33.weights, bf16[192,192]{1,0:T(8,128)(2,1)S(1)} %bitcast.26, f32[64,1]{1,0:T(8,128)S(1)} %copy.24.bias2, bf16[16,64,128]{2,1,0:T(8,128)(2,1)S(1)} %select_select_fusion.center, ...), custom_call_target="tpu_custom_call" | custom-call | flops 3221225472 | bytes 6291456 | tf_op jit(solution)/shard_map/refine/pallas_call | solution.py:19
  (4 shorter events, 0.1 us)
Async XLA Ops:
  0.6 22.2 %copy-start.6 = (f32[2,64]{1,0:T(2,128)S(1)}, f32[2,64]{1,0:T(2,128)}, u32[]{:S(2)}) copy-start(f32[2,64]{1,0:T(2,128)} %param.17) | copy-start | bytes 1540
  0.6 22.2 %copy-start.7 = (s32[2]{0:T(128)S(1)}, s32[2]{0:T(128)}, u32[]{:S(2)}) copy-start(s32[2]{0:T(128)} %param.12) | copy-start | bytes 28
  0.7 22.4 %copy-start.5 = (f32[2,64]{1,0:T(2,128)S(1)}, f32[2,64]{1,0:T(2,128)}, u32[]{:S(2)}) copy-start(f32[2,64]{1,0:T(2,128)} %param.14) | copy-start | bytes 1540
  0.7 22.5 %copy-start.4 = (bf16[3,64,384]{2,1,0:T(8,128)(2,1)S(1)}, bf16[3,64,384]{2,1,0:T(8,128)(2,1)}, u32[]{:S(2)}) copy-start(bf16[3,64,384]{2,1,0:T(8,128)(2,1)} %param.15) | copy-start | bytes 442372
  0.7 24.6 %copy-start = (bf16[2,3,64,192]{3,2,1,0:T(8,128)(2,1)S(1)}, bf16[2,3,64,192]{3,2,1,0:T(8,128)(2,1)}, u32[]{:S(2)}) copy-start(bf16[2,3,64,192]{3,2,1,0:T(8,128)(2,1)} %param.13) | copy-start | bytes 442372
  2.2 11.8 %all-to-all-start = ((bf16[32,16,128]{2,1,0:T(8,128)(2,1)}), bf16[32,16,128]{2,1,0:T(8,128)(2,1)S(1)}, u32[]{:S(2)}, u32[]{:S(2)}) async-start(bf16[32,16,128]{2,1,0:T(8,128)(2,1)} %broadcast_in_dim.10), calls=%async_computation | async-start | bytes 262144 | tf_op jit(solution)/shard_map/all_to_all | solution.py:449
  10.2 5.9 %collective-permute-start.1 = (bf16[6,64,128]{2,1,0:T(8,128)(2,1)S(1)}, bf16[6,64,128]{2,1,0:T(8,128)(2,1)S(1)}, u32[]{:S(2)}, u32[]{:S(2)}) collective-permute-start(bf16[6,64,128]{2,1,0:T(8,128)(2,1)S(1)} %get-tuple-element.38), channel_id=1, source_target_pairs={{4,8},{12,16},{20,24},{8,4},{16,12},{24,20},{5,9},{13,17},{21,25},... | collective-permute-start | bytes 294920 | tf_op jit(solution)/shard_map/ppermute | solution.py:457
  12.4 3.7 %collective-permute-start = (bf16[6,64,128]{2,1,0:T(8,128)(2,1)S(1)}, bf16[6,64,128]{2,1,0:T(8,128)(2,1)S(1)}, u32[]{:S(2)}, u32[]{:S(2)}) collective-permute-start(bf16[6,64,128]{2,1,0:T(8,128)(2,1)S(1)} %get-tuple-element.39), channel_id=1, source_target_pairs={{0,4},{4,0},{8,12},{12,8},{16,20},{20,16},{24,28},{28,24},{1,5},{5... | collective-permute-start | bytes 294920 | tf_op jit(solution)/shard_map/ppermute | solution.py:456
  17.9 5.3 %collective-permute-start.2 = (bf16[5,64,128]{2,1,0:T(8,128)(2,1)S(1)}, bf16[5,64,128]{2,1,0:T(8,128)(2,1)S(1)}, u32[]{:S(2)}, u32[]{:S(2)}) collective-permute-start(bf16[5,64,128]{2,1,0:T(8,128)(2,1)S(1)} %get-tuple-element.21), channel_id=1, source_target_pairs={{0,1},{1,0},{2,3},{3,2},{4,5},{5,4},{6,7},{7,6},{8,9},{9,8},{10,11... | collective-permute-start | bytes 245768 | tf_op jit(solution)/shard_map/ppermute | solution.py:462
  18.5 6.8 %collective-permute-start.3 = (bf16[5,64,128]{2,1,0:T(8,128)(2,1)S(1)}, bf16[5,64,128]{2,1,0:T(8,128)(2,1)S(1)}, u32[]{:S(2)}, u32[]{:S(2)}) collective-permute-start(bf16[5,64,128]{2,1,0:T(8,128)(2,1)S(1)} %get-tuple-element.22), channel_id=1, source_target_pairs={{1,2},{2,1},{5,6},{6,5},{9,10},{10,9},{13,14},{14,13},{17,18},{18,... | collective-permute-start | bytes 245768 | tf_op jit(solution)/shard_map/ppermute | solution.py:462
  35.0 31.8 %collective-permute-start.5 = (bf16[16,64,128]{2,1,0:T(8,128)(2,1)S(1)}, bf16[16,64,128]{2,1,0:T(8,128)(2,1)}, u32[]{:S(2)}, u32[]{:S(2)}) collective-permute-start(bf16[16,64,128]{2,1,0:T(8,128)(2,1)S(1)} %get-tuple-element.24.m01), channel_id=1, source_target_pairs={{0,1},{18,4},{1,3},{19,6},{4,9},{22,12},{5,11},{23,14},{8,17},{26,... | collective-permute-start | bytes 786440 | tf_op jit(solution)/shard_map/ppermute | solution.py:520
  38.7 28.1 %collective-permute-start.7 = (bf16[16,64,128]{2,1,0:T(8,128)(2,1)S(1)}, bf16[16,64,128]{2,1,0:T(8,128)(2,1)}, u32[]{:S(2)}, u32[]{:S(2)}) collective-permute-start(bf16[16,64,128]{2,1,0:T(8,128)(2,1)S(1)} %get-tuple-element.26.m11), channel_id=1, source_target_pairs={{0,5},{18,0},{1,7},{19,2},{4,13},{22,8},{5,15},{23,10},{8,21},{26,... | collective-permute-start | bytes 786440 | tf_op jit(solution)/shard_map/ppermute | solution.py:520
  55.1 11.6 %collective-permute-start.4 = (bf16[16,64,128]{2,1,0:T(8,128)(2,1)S(1)}, bf16[16,64,128]{2,1,0:T(8,128)(2,1)S(1)}, u32[]{:S(2)}, u32[]{:S(2)}) collective-permute-start(bf16[16,64,128]{2,1,0:T(8,128)(2,1)S(1)} %get-tuple-element.23.m00), channel_id=1, source_target_pairs={{0,0},{18,5},{1,2},{19,7},{4,8},{22,13},{5,10},{23,15},{8,16},{26,... | collective-permute-start | bytes 786440 | tf_op jit(solution)/shard_map/ppermute | solution.py:520
  56.5 12.3 %collective-permute-start.6 = (bf16[16,64,128]{2,1,0:T(8,128)(2,1)S(1)}, bf16[16,64,128]{2,1,0:T(8,128)(2,1)S(1)}, u32[]{:S(2)}, u32[]{:S(2)}) collective-permute-start(bf16[16,64,128]{2,1,0:T(8,128)(2,1)S(1)} %get-tuple-element.25.m10), channel_id=1, source_target_pairs={{0,4},{18,1},{1,6},{19,3},{4,12},{22,9},{5,14},{23,11},{8,20},{26,... | collective-permute-start | bytes 786440 | tf_op jit(solution)/shard_map/ppermute | solution.py:520
  60.9 22.6 %copy-start.1 = (bf16[3,64,192]{2,1,0:T(8,128)(2,1)S(1)}, bf16[3,64,192]{2,1,0:T(8,128)(2,1)}, u32[]{:S(2)}) copy-start(bf16[3,64,192]{2,1,0:T(8,128)(2,1)} %param.16) | copy-start | bytes 221188
  64.5 12.3 %copy-start.2 = (f32[96,64,128]{2,1,0:T(8,128)}, f32[96,64,128]{2,1,0:T(8,128)S(1)}, u32[]{:S(2)}) copy-start(f32[96,64,128]{2,1,0:T(8,128)S(1)} %get-tuple-element.36.row_terms) | copy-start | bytes 9437188
  69.8 5.9 %collective-permute-start.9 = (bf16[6,64,128]{2,1,0:T(8,128)(2,1)S(1)}, bf16[6,64,128]{2,1,0:T(8,128)(2,1)S(1)}, u32[]{:S(2)}, u32[]{:S(2)}) collective-permute-start(bf16[6,64,128]{2,1,0:T(8,128)(2,1)S(1)} %get-tuple-element.40), channel_id=1, source_target_pairs={{4,8},{12,16},{20,24},{8,4},{16,12},{24,20},{5,9},{13,17},{21,25},... | collective-permute-start | bytes 294920 | tf_op jit(solution)/shard_map/ppermute | solution.py:457
  71.7 4.0 %collective-permute-start.8 = (bf16[6,64,128]{2,1,0:T(8,128)(2,1)S(1)}, bf16[6,64,128]{2,1,0:T(8,128)(2,1)S(1)}, u32[]{:S(2)}, u32[]{:S(2)}) collective-permute-start(bf16[6,64,128]{2,1,0:T(8,128)(2,1)S(1)} %get-tuple-element.41), channel_id=1, source_target_pairs={{0,4},{4,0},{8,12},{12,8},{16,20},{20,16},{24,28},{28,24},{1,5},{5... | collective-permute-start | bytes 294920 | tf_op jit(solution)/shard_map/ppermute | solution.py:456
  76.7 4.9 %collective-permute-start.10 = (bf16[7,64,128]{2,1,0:T(8,128)(2,1)S(1)}, bf16[7,64,128]{2,1,0:T(8,128)(2,1)S(1)}, u32[]{:S(2)}, u32[]{:S(2)}) collective-permute-start(bf16[7,64,128]{2,1,0:T(8,128)(2,1)S(1)} %get-tuple-element.34), channel_id=1, source_target_pairs={{0,1},{1,0},{2,3},{3,2},{4,5},{5,4},{6,7},{7,6},{8,9},{9,8},{10,11... | collective-permute-start | bytes 344072 | tf_op jit(solution)/shard_map/ppermute | solution.py:462
  76.8 6.7 %collective-permute-start.11 = (bf16[7,64,128]{2,1,0:T(8,128)(2,1)S(1)}, bf16[7,64,128]{2,1,0:T(8,128)(2,1)S(1)}, u32[]{:S(2)}, u32[]{:S(2)}) collective-permute-start(bf16[7,64,128]{2,1,0:T(8,128)(2,1)S(1)} %get-tuple-element.35), channel_id=1, source_target_pairs={{1,2},{2,1},{5,6},{6,5},{9,10},{10,9},{13,14},{14,13},{17,18},{18,... | collective-permute-start | bytes 344072 | tf_op jit(solution)/shard_map/ppermute | solution.py:462
  83.5 1.9 %copy-start.3 = (f32[96,64,128]{2,1,0:T(8,128)S(1)}, f32[96,64,128]{2,1,0:T(8,128)}, u32[]{:S(2)}) copy-start(f32[96,64,128]{2,1,0:T(8,128)} %copy-done.2) | copy-start | bytes 9437188

commit v4 on v3

--- a/solution.py
+++ b/solution.py
@@ -135,7 +135,7 @@
         out[row] = dot(weights, taps[row])
         return carry
 
-    lax.fori_loop(0, count, one, 0, unroll=4)
+    lax.fori_loop(0, count, one, 0, unroll=8)
 
 
 def combine(parts, row, spacing):
@@ -313,7 +313,7 @@
     terms[0] = taps[0] + taps[1] + taps[2] + bias[...]
     terms[1] = taps[1] + jnp.where(at_left, taps[2], taps[0]) + bias[...]
     for n in range(row_terms.shape[0]):
-        row_terms[n] = jnp.where(inside_taps, terms[0, :, n : n + 1], terms[1, :, n : n + 1])
+        row_terms[n] = jnp.where(inside_taps, terms[0, :, n : n + 1], terms[1, :, n : n + 1]).astype(bf16)
     for v in range(2):
         across = dot(col_weights[...], stacked(col_start - 24 + v, 2, 4))
         for a in range(3):
@@ -392,7 +392,7 @@
                 for v in range(2)
             ]
             for u in range(2):
-                own = row_terms[2 * k + u]
+                own = row_terms[2 * k + u].astype(f32)
                 h = [(jnp.maximum(s + own, 0.0) * mask).astype(bf16) for s in sums]
                 blocks.append(jnp.concatenate(h, axis=1))
         moved = dot(jnp.concatenate(blocks, axis=0), spread).astype(bf16)
@@ -531,7 +531,7 @@
     fine_parts = parts[..., channels:]
     row_terms, col_terms = call(
         fine_kernel,
-        (struct((rows + 32, channels, 128), f32), struct((2, 3, channels, 128), f32)),
+        (struct((rows + 32, channels, 128)), struct((2, 3, channels, 128), f32)),
         [pltpu.VMEM((2, channels, 128), f32)],
         (1 << 28, 4 << 20),
         "fine",

time: 97.9 us -> 94.6 us (0.966)
  Pallas kernels: 39.5 us -> 37.1 us
  local copies, waits for them, and re-layouts: 5.91 us -> 4.04 us
    pallas_call x7, Pallas kernels: 39.5 us -> 37.1 us  [run(): pl.pallas_call(body, out_shape=outs, in_specs=[SMEM] + [VMEM] * (len(args...]
    unnamed x17 -> x13, local copies, waits for them, and re-layouts: 3.83 us -> 1.95 us
  transfers between devices with their start and end apart: 13 -> 13, of which waited for: 7 -> 6; matrix products, arithmetic and copies ran while one was open for 3% -> 4% of each run, Pallas kernels for 15% -> 15%
where the time goes in v4:
time: 94.6 us; the launch traced here: 94.2 us
  Pallas kernels  37.1 us (39%)
  starting transfers between devices  35.2 us (37%)
  waiting for transfers between devices  15 us (16%)
  local copies, waits for them, and re-layouts  4.04 us (4%)
  other arithmetic  1.9 us (2%)
  between operations  0.97 us (1%)
    pallas_call x7, Pallas kernels, run(): pl.pallas_call(body, out_shape=outs, in_specs=[SMEM] + [VMEM] * (len(args...  37.1 us
    ppermute x4, starting transfers between devices, per_device(): lax.ppermute(messages[2 * u + v], ('row', 'col'), pairs)  16.5 us
    ppermute x4, starting transfers between devices, col_swap(): return (lax.ppermute(a, 'col', first), lax.ppermute(b, 'col', second))  6.95 us
    ppermute x4, waiting for transfers between devices, col_swap(): return (lax.ppermute(a, 'col', first), lax.ppermute(b, 'col', second))  6.74 us
    ppermute x2, waiting for transfers between devices, row_swap(): lax.ppermute(jnp.where(odd_row, bottom, top), 'row', second)  6.09 us
    all_to_all x1, starting transfers between devices, per_device(): lax.all_to_all(spread, ('row', 'col'), split_axis=0, concat_axis=0, tiled...  6.02 us
    ppermute x2, starting transfers between devices, row_swap(): lax.ppermute(jnp.where(odd_row, bottom, top), 'row', second)  4.24 us
    ppermute x4, waiting for transfers between devices, per_device(): lax.ppermute(messages[2 * u + v], ('row', 'col'), pairs)  2.13 us
  transfers between devices with their start and end apart: 13, of which 6 were waited for; matrix products, arithmetic and copies ran while one was open for 4% of the time, Pallas kernels for 15%

profile of v4, /device:TPU:10, one launch (start us, length us, event | category | flops | bytes accessed | tf_op | source)
XLA Modules:
  0.0 94.2 jit_solution(14567944175725138416)
XLA Ops:
  0.6 0.8 maximum_bitcast_fusion
  1.4 0.7 broadcast_in_dim.10
  2.1 6.0 %all-to-all-start = ((bf16[32,16,128]{2,1,0:T(8,128)(2,1)}), bf16[32,16,128]{2,1,0:T(8,128)(2,1)S(1)}, u32[]{:S(2)}, u32[]{:S(2)}) async-start(bf16[32,16,128]{2,1,0:T(8,128)(2,1)} %broadcast_in_dim.10), calls=%async_computation | async-start | bytes 262144 | tf_op jit(solution)/shard_map/all_to_all | solution.py:449
  8.1 0.0 copy-start.4
  8.1 0.0 copy-start.5
  8.2 1.9 %copy.26 = bf16[64,64,128]{2,0,1:T(8,128)(2,1)S(1)} copy(bf16[64,64,128]{2,1,0:T(8,128)(2,1)} %param.11) | data formatting | bytes 2097152 | tf_op args[2]
  10.1 0.0 copy-start.3
  10.1 0.0 copy-start.2
  10.1 0.0 copy-start
  10.1 2.3 %collective-permute-start.1 = (bf16[6,64,128]{2,1,0:T(8,128)(2,1)S(1)}, bf16[6,64,128]{2,1,0:T(8,128)(2,1)S(1)}, u32[]{:S(2)}, u32[]{:S(2)}) collective-permute-start(bf16[6,64,128]{2,1,0:T(8,128)(2,1)S(1)} %get-tuple-element.38), channel_id=1, source_target_pairs={{4,8},{12,16},{20,24},{8,4},{16,12},{24,20},{5,9},{13,17},{21,25},... | collective-permute-start | bytes 294920 | tf_op jit(solution)/shard_map/ppermute | solution.py:457
  12.5 1.4 %collective-permute-start = (bf16[6,64,128]{2,1,0:T(8,128)(2,1)S(1)}, bf16[6,64,128]{2,1,0:T(8,128)(2,1)S(1)}, u32[]{:S(2)}, u32[]{:S(2)}) collective-permute-start(bf16[6,64,128]{2,1,0:T(8,128)(2,1)S(1)} %get-tuple-element.39), channel_id=1, source_target_pairs={{0,4},{4,0},{8,12},{12,8},{16,20},{20,16},{24,28},{28,24},{1,5},{5... | collective-permute-start | bytes 294920 | tf_op jit(solution)/shard_map/ppermute | solution.py:456
  13.8 0.1 stack.11.pos
  13.9 0.0 all-to-all-done
  13.9 0.1 copy.18
  14.0 2.2 %collective-permute-done.1.row_b = bf16[6,64,128]{2,1,0:T(8,128)(2,1)S(1)} collective-permute-done((bf16[6,64,128]{2,1,0:T(8,128)(2,1)S(1)}, bf16[6,64,128]{2,1,0:T(8,128)(2,1)S(1)}, u32[]{:S(2)}, u32[]{:S(2)}) %collective-permute-start.1) | collective-permute-done | bytes 98336 | tf_op jit(solution)/shard_map/ppermute | solution.py:457
  16.2 0.0 collective-permute-done.row_a
  16.2 1.8 %pair.1 = (bf16[76,64,128]{2,1,0:T(8,128)(2,1)S(1)}, bf16[5,64,128]{2,1,0:T(8,128)(2,1)S(1)}, bf16[5,64,128]{2,1,0:T(8,128)(2,1)S(1)}) custom-call(s32[5]{0:T(128)S(1)} %stack.11.pos, bf16[128,512]{1,0:T(8,128)(2,1)S(1)} %bitcast.22, bf16[64,64,128]{2,1,0:T(8,128)(2,1)S(1)} %bitcast.21, bf16[6,64,128]{2,1,0:T(8,128)(2,1)S(1)} %collective-permute-done.row_a, ...), custom_call_target="tpu_custom_call" | custom-call | flops 268435456 | bytes 4194304 | tf_op jit(solution)/shard_map/pair/pallas_call | solution.py:19
  18.0 0.6 collective-permute-start.2
  18.6 4.3 %collective-permute-start.3 = (bf16[5,64,128]{2,1,0:T(8,128)(2,1)S(1)}, bf16[5,64,128]{2,1,0:T(8,128)(2,1)S(1)}, u32[]{:S(2)}, u32[]{:S(2)}) collective-permute-start(bf16[5,64,128]{2,1,0:T(8,128)(2,1)S(1)} %get-tuple-element.22), channel_id=1, source_target_pairs={{1,2},{2,1},{5,6},{6,5},{9,10},{10,9},{13,14},{14,13},{17,18},{18,... | collective-permute-start | bytes 245768 | tf_op jit(solution)/shard_map/ppermute | solution.py:462
  22.9 0.0 copy-done.4
  23.0 0.0 copy-done.5
  23.0 0.1 copy.23.bias
  23.1 0.0 copy-done.3
  23.1 0.1 copy.20.bias
  23.2 0.0 copy-done.2
  23.3 0.0 collective-permute-done.2.col_a
  23.3 2.1 %collective-permute-done.3.col_b = bf16[5,64,128]{2,1,0:T(8,128)(2,1)S(1)} collective-permute-done((bf16[5,64,128]{2,1,0:T(8,128)(2,1)S(1)}, bf16[5,64,128]{2,1,0:T(8,128)(2,1)S(1)}, u32[]{:S(2)}, u32[]{:S(2)}) %collective-permute-start.3) | collective-permute-done | bytes 81952 | tf_op jit(solution)/shard_map/ppermute | solution.py:462
  25.4 0.0 copy-done
  25.4 9.3 %tile1.1 = (bf16[16,64,128]{2,1,0:T(8,128)(2,1)S(1)}, bf16[16,64,128]{2,1,0:T(8,128)(2,1)S(1)}) custom-call(s32[5]{0:T(128)S(1)} %stack.11.pos, bf16[2,192,192]{2,1,0:T(8,128)(2,1)S(1)} %bitcast.24, f32[2,64,1]{2,1,0:T(8,128)S(1)} %copy.20.bias, bf16[76,64,128]{2,1,0:T(8,128)(2,1)S(1)} %get-tuple-element.20.pair, ...), custom_call_target="tpu_custom_call" | custom-call | flops 3221225472 | bytes 3145728 | tf_op jit(solution)/shard_map/tile1/pallas_call | solution.py:19
  34.7 3.7 %collective-permute-start.5 = (bf16[16,64,128]{2,1,0:T(8,128)(2,1)S(1)}, bf16[16,64,128]{2,1,0:T(8,128)(2,1)}, u32[]{:S(2)}, u32[]{:S(2)}) collective-permute-start(bf16[16,64,128]{2,1,0:T(8,128)(2,1)S(1)} %get-tuple-element.24.m01), channel_id=1, source_target_pairs={{0,1},{18,4},{1,3},{19,6},{4,9},{22,12},{5,11},{23,14},{8,17},{26,... | collective-permute-start | bytes 786440 | tf_op jit(solution)/shard_map/ppermute | solution.py:520
  38.3 6.8 %collective-permute-start.7 = (bf16[16,64,128]{2,1,0:T(8,128)(2,1)S(1)}, bf16[16,64,128]{2,1,0:T(8,128)(2,1)}, u32[]{:S(2)}, u32[]{:S(2)}) collective-permute-start(bf16[16,64,128]{2,1,0:T(8,128)(2,1)S(1)} %get-tuple-element.26.m11), channel_id=1, source_target_pairs={{0,5},{18,0},{1,7},{19,2},{4,13},{22,8},{5,15},{23,10},{8,21},{26,... | collective-permute-start | bytes 786440 | tf_op jit(solution)/shard_map/ppermute | solution.py:520
  45.1 9.3 %tile0.1 = (bf16[16,64,128]{2,1,0:T(8,128)(2,1)S(1)}, bf16[16,64,128]{2,1,0:T(8,128)(2,1)S(1)}) custom-call(s32[5]{0:T(128)S(1)} %stack.11.pos, bf16[2,192,192]{2,1,0:T(8,128)(2,1)S(1)} %bitcast.25, f32[2,64,1]{2,1,0:T(8,128)S(1)} %copy.20.bias, bf16[76,64,128]{2,1,0:T(8,128)(2,1)S(1)} %get-tuple-element.20.pair, ...), custom_call_target="tpu_custom_call" | custom-call | flops 3221225472 | bytes 3145728 | tf_op jit(solution)/shard_map/tile0/pallas_call | solution.py:19
  54.4 2.0 %collective-permute-start.4 = (bf16[16,64,128]{2,1,0:T(8,128)(2,1)S(1)}, bf16[16,64,128]{2,1,0:T(8,128)(2,1)}, u32[]{:S(2)}, u32[]{:S(2)}) collective-permute-start(bf16[16,64,128]{2,1,0:T(8,128)(2,1)S(1)} %get-tuple-element.23.m00), channel_id=1, source_target_pairs={{0,0},{18,5},{1,2},{19,7},{4,8},{22,13},{5,10},{23,15},{8,16},{26,... | collective-permute-start | bytes 786440 | tf_op jit(solution)/shard_map/ppermute | solution.py:520
  56.4 4.0 %collective-permute-start.6 = (bf16[16,64,128]{2,1,0:T(8,128)(2,1)S(1)}, bf16[16,64,128]{2,1,0:T(8,128)(2,1)}, u32[]{:S(2)}, u32[]{:S(2)}) collective-permute-start(bf16[16,64,128]{2,1,0:T(8,128)(2,1)S(1)} %get-tuple-element.25.m10), channel_id=1, source_target_pairs={{0,4},{18,1},{1,6},{19,3},{4,12},{22,9},{5,14},{23,11},{8,20},{26,... | collective-permute-start | bytes 786440 | tf_op jit(solution)/shard_map/ppermute | solution.py:520
  60.5 0.2 fusion
  60.7 0.2 reshape.33.weights
  60.8 0.2 reshape.32.col_weights
  61.0 0.2 copy.22
  61.2 0.2 reshape.31.row_weights
  61.3 2.4 %fine.1 = (bf16[96,64,128]{2,1,0:T(8,128)(2,1)S(1)}, f32[2,3,64,128]{3,2,1,0:T(8,128)S(1)}) custom-call(s32[5]{0:T(128)S(1)} %stack.11.pos, bf16[192,192]{1,0:T(8,128)(2,1)S(1)} %reshape.31.row_weights, bf16[192,192]{1,0:T(8,128)(2,1)S(1)} %reshape.32.col_weights, f32[64,1]{1,0:T(8,128)S(1)} %copy.23.bias, bf16[128,512]{1,0:T(8,128)(2,1)S(1)} %bitcast.23), custom_call_target="tpu_custom_call" | custom-call | flops 268435456 | bytes 4194304 | tf_op jit(solution)/shard_map/fine/pallas_call | solution.py:19
  63.7 2.3 %assemble.1 = bf16[64,64,128]{2,1,0:T(8,128)(2,1)} custom-call(s32[5]{0:T(128)S(1)} %stack.11.pos, bf16[16,64,128]{2,1,0:T(8,128)(2,1)S(1)} %get-tuple-element.23.m00, bf16[16,64,128]{2,1,0:T(8,128)(2,1)S(1)} %get-tuple-element.24.m01, bf16[16,64,128]{2,1,0:T(8,128)(2,1)S(1)} %get-tuple-element.25.m10, bf16[16,64,128]{2,1,0:T(8,128)(2,1)S(1)} %get-tuple-element.26.m11), custom_call_target="tpu_custom_call" | custom-call | flops 1048576 | bytes 2097152 | tf_op jit(solution)/shard_map/assemble/pallas_call | solution.py:19
  66.0 0.0 copy-start.1
  66.0 0.0 collective-permute-done.5
  66.0 0.0 collective-permute-done.7
  66.0 0.0 collective-permute-done.4
  66.0 2.1 %collective-permute-done.6 = bf16[16,64,128]{2,1,0:T(8,128)(2,1)} collective-permute-done((bf16[16,64,128]{2,1,0:T(8,128)(2,1)S(1)}, bf16[16,64,128]{2,1,0:T(8,128)(2,1)}, u32[]{:S(2)}, u32[]{:S(2)}) %collective-permute-start.6) | collective-permute-done | bytes 262176 | tf_op jit(solution)/shard_map/ppermute | solution.py:520
  68.1 1.1 %select_select_fusion.center = bf16[16,64,128]{2,1,0:T(8,128)(2,1)S(1)} fusion(bf16[16,64,128]{2,1,0:T(8,128)(2,1)} %collective-permute-done.6, bf16[16,64,128]{2,1,0:T(8,128)(2,1)} %collective-permute-done.7, bf16[16,64,128]{2,1,0:T(8,128)(2,1)} %collective-permute-done.4, bf16[16,64,128]{2,1,0:T(8,128)(2,1)} %collective-permute-done.5, pred[]{:T(512)S(6)} %eq.15, ...), kind=kLoop, calls=%fused_computation.1 | loop fusion | flops 393216 | bytes 1310723 | tf_op jit(solution)/shard_map/jit(_where)/select_n | solution.py:523
  69.2 1.9 %collective-permute-start.9 = (bf16[6,64,128]{2,1,0:T(8,128)(2,1)S(1)}, bf16[6,64,128]{2,1,0:T(8,128)(2,1)S(1)}, u32[]{:S(2)}, u32[]{:S(2)}) collective-permute-start(bf16[6,64,128]{2,1,0:T(8,128)(2,1)S(1)} %get-tuple-element.40), channel_id=1, source_target_pairs={{4,8},{12,16},{20,24},{8,4},{16,12},{24,20},{5,9},{13,17},{21,25},... | collective-permute-start | bytes 294920 | tf_op jit(solution)/shard_map/ppermute | solution.py:457
  71.2 0.1 collective-permute-start.8
  71.2 3.9 %collective-permute-done.9.row_b = bf16[6,64,128]{2,1,0:T(8,128)(2,1)S(1)} collective-permute-done((bf16[6,64,128]{2,1,0:T(8,128)(2,1)S(1)}, bf16[6,64,128]{2,1,0:T(8,128)(2,1)S(1)}, u32[]{:S(2)}, u32[]{:S(2)}) %collective-permute-start.9) | collective-permute-done | bytes 98336 | tf_op jit(solution)/shard_map/ppermute | solution.py:457
  75.2 0.0 collective-permute-done.8.row_a
  75.2 0.9 window_strips.1
  76.1 0.1 collective-permute-start.10
  76.2 1.9 %collective-permute-start.11 = (bf16[7,64,128]{2,1,0:T(8,128)(2,1)S(1)}, bf16[7,64,128]{2,1,0:T(8,128)(2,1)S(1)}, u32[]{:S(2)}, u32[]{:S(2)}) collective-permute-start(bf16[7,64,128]{2,1,0:T(8,128)(2,1)S(1)} %get-tuple-element.35), channel_id=1, source_target_pairs={{1,2},{2,1},{5,6},{6,5},{9,10},{10,9},{13,14},{14,13},{17,18},{18,... | collective-permute-start | bytes 344072 | tf_op jit(solution)/shard_map/ppermute | solution.py:462
  78.1 0.1 copy.24.bias2
  78.2 2.8 %collective-permute-done.10.col_a = bf16[7,64,128]{2,1,0:T(8,128)(2,1)S(1)} collective-permute-done((bf16[7,64,128]{2,1,0:T(8,128)(2,1)S(1)}, bf16[7,64,128]{2,1,0:T(8,128)(2,1)S(1)}, u32[]{:S(2)}, u32[]{:S(2)}) %collective-permute-start.10) | collective-permute-done | bytes 114720 | tf_op jit(solution)/shard_map/ppermute | solution.py:462
  81.0 1.9 %collective-permute-done.11.col_b = bf16[7,64,128]{2,1,0:T(8,128)(2,1)S(1)} collective-permute-done((bf16[7,64,128]{2,1,0:T(8,128)(2,1)S(1)}, bf16[7,64,128]{2,1,0:T(8,128)(2,1)S(1)}, u32[]{:S(2)}, u32[]{:S(2)}) %collective-permute-start.11) | collective-permute-done | bytes 114720 | tf_op jit(solution)/shard_map/ppermute | solution.py:462
  82.9 0.0 copy-done.1
  82.9 11.3 %refine.1 = bf16[64,64,128]{2,1,0:T(8,128)(2,1)} custom-call(s32[5]{0:T(128)S(1)} %stack.11.pos, bf16[192,192]{1,0:T(8,128)(2,1)S(1)} %reshape.33.weights, bf16[192,192]{1,0:T(8,128)(2,1)S(1)} %bitcast.26, f32[64,1]{1,0:T(8,128)S(1)} %copy.24.bias2, bf16[16,64,128]{2,1,0:T(8,128)(2,1)S(1)} %select_select_fusion.center, ...), custom_call_target="tpu_custom_call" | custom-call | flops 3221225472 | bytes 6291456 | tf_op jit(solution)/shard_map/refine/pallas_call | solution.py:19
  (4 shorter events, 0.1 us)
Async XLA Ops:
  2.1 11.8 %all-to-all-start = ((bf16[32,16,128]{2,1,0:T(8,128)(2,1)}), bf16[32,16,128]{2,1,0:T(8,128)(2,1)S(1)}, u32[]{:S(2)}, u32[]{:S(2)}) async-start(bf16[32,16,128]{2,1,0:T(8,128)(2,1)} %broadcast_in_dim.10), calls=%async_computation | async-start | bytes 262144 | tf_op jit(solution)/shard_map/all_to_all | solution.py:449
  8.1 14.8 %copy-start.4 = (f32[2,64]{1,0:T(2,128)S(1)}, f32[2,64]{1,0:T(2,128)}, u32[]{:S(2)}) copy-start(f32[2,64]{1,0:T(2,128)} %param.17) | copy-start | bytes 1540
  8.1 14.8 %copy-start.5 = (s32[2]{0:T(128)S(1)}, s32[2]{0:T(128)}, u32[]{:S(2)}) copy-start(s32[2]{0:T(128)} %param.12) | copy-start | bytes 28
  10.1 13.1 %copy-start.3 = (f32[2,64]{1,0:T(2,128)S(1)}, f32[2,64]{1,0:T(2,128)}, u32[]{:S(2)}) copy-start(f32[2,64]{1,0:T(2,128)} %param.14) | copy-start | bytes 1540
  10.1 13.2 %copy-start.2 = (bf16[3,64,384]{2,1,0:T(8,128)(2,1)S(1)}, bf16[3,64,384]{2,1,0:T(8,128)(2,1)}, u32[]{:S(2)}) copy-start(bf16[3,64,384]{2,1,0:T(8,128)(2,1)} %param.15) | copy-start | bytes 442372
  10.1 15.3 %copy-start = (bf16[2,3,64,192]{3,2,1,0:T(8,128)(2,1)S(1)}, bf16[2,3,64,192]{3,2,1,0:T(8,128)(2,1)}, u32[]{:S(2)}) copy-start(bf16[2,3,64,192]{3,2,1,0:T(8,128)(2,1)} %param.13) | copy-start | bytes 442372
  10.1 6.1 %collective-permute-start.1 = (bf16[6,64,128]{2,1,0:T(8,128)(2,1)S(1)}, bf16[6,64,128]{2,1,0:T(8,128)(2,1)S(1)}, u32[]{:S(2)}, u32[]{:S(2)}) collective-permute-start(bf16[6,64,128]{2,1,0:T(8,128)(2,1)S(1)} %get-tuple-element.38), channel_id=1, source_target_pairs={{4,8},{12,16},{20,24},{8,4},{16,12},{24,20},{5,9},{13,17},{21,25},... | collective-permute-start | bytes 294920 | tf_op jit(solution)/shard_map/ppermute | solution.py:457
  12.5 3.7 %collective-permute-start = (bf16[6,64,128]{2,1,0:T(8,128)(2,1)S(1)}, bf16[6,64,128]{2,1,0:T(8,128)(2,1)S(1)}, u32[]{:S(2)}, u32[]{:S(2)}) collective-permute-start(bf16[6,64,128]{2,1,0:T(8,128)(2,1)S(1)} %get-tuple-element.39), channel_id=1, source_target_pairs={{0,4},{4,0},{8,12},{12,8},{16,20},{20,16},{24,28},{28,24},{1,5},{5... | collective-permute-start | bytes 294920 | tf_op jit(solution)/shard_map/ppermute | solution.py:456
  18.0 5.3 %collective-permute-start.2 = (bf16[5,64,128]{2,1,0:T(8,128)(2,1)S(1)}, bf16[5,64,128]{2,1,0:T(8,128)(2,1)S(1)}, u32[]{:S(2)}, u32[]{:S(2)}) collective-permute-start(bf16[5,64,128]{2,1,0:T(8,128)(2,1)S(1)} %get-tuple-element.21), channel_id=1, source_target_pairs={{0,1},{1,0},{2,3},{3,2},{4,5},{5,4},{6,7},{7,6},{8,9},{9,8},{10,11... | collective-permute-start | bytes 245768 | tf_op jit(solution)/shard_map/ppermute | solution.py:462
  18.6 6.8 %collective-permute-start.3 = (bf16[5,64,128]{2,1,0:T(8,128)(2,1)S(1)}, bf16[5,64,128]{2,1,0:T(8,128)(2,1)S(1)}, u32[]{:S(2)}, u32[]{:S(2)}) collective-permute-start(bf16[5,64,128]{2,1,0:T(8,128)(2,1)S(1)} %get-tuple-element.22), channel_id=1, source_target_pairs={{1,2},{2,1},{5,6},{6,5},{9,10},{10,9},{13,14},{14,13},{17,18},{18,... | collective-permute-start | bytes 245768 | tf_op jit(solution)/shard_map/ppermute | solution.py:462
  34.7 31.3 %collective-permute-start.5 = (bf16[16,64,128]{2,1,0:T(8,128)(2,1)S(1)}, bf16[16,64,128]{2,1,0:T(8,128)(2,1)}, u32[]{:S(2)}, u32[]{:S(2)}) collective-permute-start(bf16[16,64,128]{2,1,0:T(8,128)(2,1)S(1)} %get-tuple-element.24.m01), channel_id=1, source_target_pairs={{0,1},{18,4},{1,3},{19,6},{4,9},{22,12},{5,11},{23,14},{8,17},{26,... | collective-permute-start | bytes 786440 | tf_op jit(solution)/shard_map/ppermute | solution.py:520
  38.3 27.6 %collective-permute-start.7 = (bf16[16,64,128]{2,1,0:T(8,128)(2,1)S(1)}, bf16[16,64,128]{2,1,0:T(8,128)(2,1)}, u32[]{:S(2)}, u32[]{:S(2)}) collective-permute-start(bf16[16,64,128]{2,1,0:T(8,128)(2,1)S(1)} %get-tuple-element.26.m11), channel_id=1, source_target_pairs={{0,5},{18,0},{1,7},{19,2},{4,13},{22,8},{5,15},{23,10},{8,21},{26,... | collective-permute-start | bytes 786440 | tf_op jit(solution)/shard_map/ppermute | solution.py:520
  54.4 11.6 %collective-permute-start.4 = (bf16[16,64,128]{2,1,0:T(8,128)(2,1)S(1)}, bf16[16,64,128]{2,1,0:T(8,128)(2,1)}, u32[]{:S(2)}, u32[]{:S(2)}) collective-permute-start(bf16[16,64,128]{2,1,0:T(8,128)(2,1)S(1)} %get-tuple-element.23.m00), channel_id=1, source_target_pairs={{0,0},{18,5},{1,2},{19,7},{4,8},{22,13},{5,10},{23,15},{8,16},{26,... | collective-permute-start | bytes 786440 | tf_op jit(solution)/shard_map/ppermute | solution.py:520
  56.4 11.7 %collective-permute-start.6 = (bf16[16,64,128]{2,1,0:T(8,128)(2,1)S(1)}, bf16[16,64,128]{2,1,0:T(8,128)(2,1)}, u32[]{:S(2)}, u32[]{:S(2)}) collective-permute-start(bf16[16,64,128]{2,1,0:T(8,128)(2,1)S(1)} %get-tuple-element.25.m10), channel_id=1, source_target_pairs={{0,4},{18,1},{1,6},{19,3},{4,12},{22,9},{5,14},{23,11},{8,20},{26,... | collective-permute-start | bytes 786440 | tf_op jit(solution)/shard_map/ppermute | solution.py:520
  66.0 16.9 %copy-start.1 = (bf16[3,64,192]{2,1,0:T(8,128)(2,1)S(1)}, bf16[3,64,192]{2,1,0:T(8,128)(2,1)}, u32[]{:S(2)}) copy-start(bf16[3,64,192]{2,1,0:T(8,128)(2,1)} %param.16) | copy-start | bytes 221188
  69.2 5.9 %collective-permute-start.9 = (bf16[6,64,128]{2,1,0:T(8,128)(2,1)S(1)}, bf16[6,64,128]{2,1,0:T(8,128)(2,1)S(1)}, u32[]{:S(2)}, u32[]{:S(2)}) collective-permute-start(bf16[6,64,128]{2,1,0:T(8,128)(2,1)S(1)} %get-tuple-element.40), channel_id=1, source_target_pairs={{4,8},{12,16},{20,24},{8,4},{16,12},{24,20},{5,9},{13,17},{21,25},... | collective-permute-start | bytes 294920 | tf_op jit(solution)/shard_map/ppermute | solution.py:457
  71.2 4.0 %collective-permute-start.8 = (bf16[6,64,128]{2,1,0:T(8,128)(2,1)S(1)}, bf16[6,64,128]{2,1,0:T(8,128)(2,1)S(1)}, u32[]{:S(2)}, u32[]{:S(2)}) collective-permute-start(bf16[6,64,128]{2,1,0:T(8,128)(2,1)S(1)} %get-tuple-element.41), channel_id=1, source_target_pairs={{0,4},{4,0},{8,12},{12,8},{16,20},{20,16},{24,28},{28,24},{1,5},{5... | collective-permute-start | bytes 294920 | tf_op jit(solution)/shard_map/ppermute | solution.py:456
  76.1 4.9 %collective-permute-start.10 = (bf16[7,64,128]{2,1,0:T(8,128)(2,1)S(1)}, bf16[7,64,128]{2,1,0:T(8,128)(2,1)S(1)}, u32[]{:S(2)}, u32[]{:S(2)}) collective-permute-start(bf16[7,64,128]{2,1,0:T(8,128)(2,1)S(1)} %get-tuple-element.34), channel_id=1, source_target_pairs={{0,1},{1,0},{2,3},{3,2},{4,5},{5,4},{6,7},{7,6},{8,9},{9,8},{10,11... | collective-permute-start | bytes 344072 | tf_op jit(solution)/shard_map/ppermute | solution.py:462
  76.2 6.7 %collective-permute-start.11 = (bf16[7,64,128]{2,1,0:T(8,128)(2,1)S(1)}, bf16[7,64,128]{2,1,0:T(8,128)(2,1)S(1)}, u32[]{:S(2)}, u32[]{:S(2)}) collective-permute-start(bf16[7,64,128]{2,1,0:T(8,128)(2,1)S(1)} %get-tuple-element.35), channel_id=1, source_target_pairs={{1,2},{2,1},{5,6},{6,5},{9,10},{10,9},{13,14},{14,13},{17,18},{18,... | collective-permute-start | bytes 344072 | tf_op jit(solution)/shard_map/ppermute | solution.py:462
